TPU v7x, 32 devices: a whole 2x2x4 slice. The times are simulated.
32 devices in a mesh: member: 4 (over y, x), lat: 8 (over z, core).
Axes of the slice: x: 2, y: 2, z: 4, core: 2. Of those that a mesh axis runs over, the one named last changes fastest.
Arguments:
- ensemble_starting_fields: bfloat16 [4, 256, 512, 384], P('member', 'lat'), may hold values from -6 to 6
- observed: bfloat16 [256, 512, 384], P('lat'), may hold values from -6 to 6
- wave_of_slot: int32 [256], replicated, may hold values from 0 to 255, each once
- leg_forward: bfloat16 [256, 256, 256], P('lat'), may hold values from -0.375 to 0.375
- leg_inverse: bfloat16 [256, 256, 256], P('lat'), may hold values from -0.375 to 0.375
- spec_filter: float32 [2, 256, 384], replicated, may hold values from -5 to 5
- gain_first: float32 [384], replicated, may hold values from 0.5 to 1.5
- gain_second: float32 [384], replicated, may hold values from 0.5 to 1.5
- weight_in: bfloat16 [384, 768], replicated, may hold values from -0.3125 to 0.3125
- weight_out: bfloat16 [768, 384], replicated, may hold values from -0.21875 to 0.21875
Outputs:
- predicted_field: bfloat16 [4, 256, 512, 384], P('member', 'lat')
- proper_loss_slope: bfloat16 [4, 256, 512, 384], P('member', 'lat')
Inputs may be any that keep to these rules, and one draw needn't show every extreme that they name: `wave_of_slot`: every wavenumber 0 to 255 sits in exactly one slot.
All inputs are finite; a program needn't handle non-finite values.
Results may differ from a plain program's by a relative error of at most 0.013.
Values may be sent and summed in bfloat16 or wider, within the bound.
No kernel may reach another device: no remote copies, remote signals or barrier semaphores. Data moves between devices by JAX's collectives and lax.ppermute only.
A program may use at most 192 MiB of HBM per device.

v0:
```python
import math

import jax
import jax.numpy as jnp
from jax import lax
from jax.sharding import PartitionSpec as P

EPS_NORM = 1e-05
EPS_DIST = 1e-06


def layer_norm(values, scales):
    average = jnp.mean(values, -1, keepdims=True)
    centred = values - average
    spread = jnp.mean(centred * centred, -1, keepdims=True)
    return centred * lax.rsqrt(spread + EPS_NORM) * scales


def distance(first, second):
    return jnp.sqrt(jnp.mean(jnp.square(first - second), -1, keepdims=True) + EPS_DIST)


def dft_tables(numbers, length):
    columns = jnp.arange(length, dtype=jnp.int32)
    phases = numbers[:, None] * columns[None, :] % length
    angles = phases.astype(jnp.float32) * (2.0 * math.pi / length)
    return (jnp.cos(angles), jnp.sin(angles))


def split_table(table):
    table_high = table.astype(jnp.bfloat16)
    table_low = (table - table_high.astype(jnp.float32)).astype(jnp.bfloat16)
    return (table_high, table_low)


def member_grad(own, others, target, divisor):
    pulled = jnp.zeros_like(own)
    for other in others:
        pulled = pulled + (own - other) / distance(own, other)
    return (own - target) / distance(own, target) - pulled / divisor


def local(
    ensemble_starting_fields,
    observed,
    wave_of_slot,
    leg_forward,
    leg_inverse,
    spec_filter,
    gain_first,
    gain_second,
    weight_in,
    weight_out,
):
    lat_rows = ensemble_starting_fields.shape[1]
    length = ensemble_starting_fields.shape[2]
    channels = ensemble_starting_fields.shape[3]
    waves_all = wave_of_slot.shape[0]
    slots = leg_forward.shape[0]
    degrees = leg_forward.shape[1]
    values = ensemble_starting_fields[0].astype(jnp.float32)
    normed = layer_norm(values, gain_first).astype(jnp.bfloat16)
    cosines, sines = dft_tables(wave_of_slot, length)
    fwd_table = jnp.stack([cosines / length, -sines / length], 1).reshape(2 * waves_all, length)
    fwd_high, fwd_low = split_table(fwd_table)
    analysis = jnp.einsum("kj,ljc->klc", fwd_high, normed, preferred_element_type=jnp.float32)
    analysis = analysis + jnp.einsum(
        "kj,ljc->klc", fwd_low, normed, preferred_element_type=jnp.float32
    )
    analysis = analysis.astype(jnp.bfloat16).reshape(waves_all, 2, lat_rows, channels)
    spectra = lax.all_to_all(analysis, "lat", split_axis=0, concat_axis=2, tiled=True)
    local_waves = lax.dynamic_slice_in_dim(wave_of_slot, lax.axis_index("lat") * slots, slots)
    order = jnp.arange(degrees, dtype=jnp.int32)
    retain = (order[None, :] >= local_waves[:, None]).astype(jnp.float32)[:, None, :, None]
    filt_real = spec_filter[0]
    filt_imag = spec_filter[1]
    coeffs = (
        jnp.einsum("sln,srnc->srlc", leg_forward, spectra, preferred_element_type=jnp.float32)
        * retain
    )
    real_part = coeffs[:, 0]
    imag_part = coeffs[:, 1]
    filtered = jnp.stack(
        [
            real_part * filt_real - imag_part * filt_imag,
            real_part * filt_imag + imag_part * filt_real,
        ],
        1,
    ).astype(jnp.bfloat16)
    synthesis = jnp.einsum(
        "snl,srlc->srnc", leg_inverse, filtered, preferred_element_type=jnp.float32
    )
    synthesis = synthesis.astype(jnp.bfloat16)
    returned = lax.all_to_all(synthesis, "lat", split_axis=2, concat_axis=0, tiled=True)
    returned = returned.reshape(2 * waves_all, lat_rows, channels)
    weights_m = jnp.where(wave_of_slot == 0, 1.0, 2.0).astype(jnp.float32)[:, None]
    inv_table = jnp.stack([weights_m * cosines, -weights_m * sines], 1).reshape(
        2 * waves_all, length
    )
    inv_high, inv_low = split_table(inv_table)
    spectral = jnp.einsum("kj,klc->ljc", inv_high, returned, preferred_element_type=jnp.float32)
    spectral = spectral + jnp.einsum(
        "kj,klc->ljc", inv_low, returned, preferred_element_type=jnp.float32
    )
    harmonic_damped_field = values + spectral
    normed_two = (
        layer_norm(harmonic_damped_field, gain_second)
        .astype(jnp.bfloat16)
        .reshape(lat_rows * length, channels)
    )
    hidden = jax.nn.gelu(jnp.dot(normed_two, weight_in, preferred_element_type=jnp.float32)).astype(
        jnp.bfloat16
    )
    feedforward_result = jnp.dot(hidden, weight_out, preferred_element_type=jnp.float32).reshape(
        lat_rows, length, channels
    )
    predicted_field = (harmonic_damped_field + feedforward_result).astype(jnp.bfloat16)[None]
    members = lax.axis_size("member")
    gathered_fields = lax.all_to_all(
        predicted_field, "member", split_axis=2, concat_axis=0, tiled=True
    )
    block_cols = length // members
    first_col = lax.axis_index("member") * block_cols
    target = lax.dynamic_slice_in_dim(observed, first_col, block_cols, 1).astype(jnp.float32)
    others = [gathered_fields[member_index].astype(jnp.float32) for member_index in range(members)]
    grads = [
        member_grad(others[member_index], others, target, members - 1)
        for member_index in range(members)
    ]
    grads = jnp.stack(grads, 0).astype(jnp.bfloat16)
    proper_loss_slope = lax.all_to_all(grads, "member", split_axis=0, concat_axis=2, tiled=True)
    return (predicted_field, proper_loss_slope)


def solution(mesh):
    in_specs = (
        P("member", "lat", None, None),
        P("lat", None, None),
        P(),
        P("lat", None, None),
        P("lat", None, None),
        P(),
        P(),
        P(),
        P(),
        P(),
    )
    out_specs = (P("member", "lat", None, None), P("member", "lat", None, None))
    return jax.shard_map(local, mesh=mesh, in_specs=in_specs, out_specs=out_specs, check_vma=False)
```

profile of v0, /device:TPU:0, one launch (start us, length us, event | category | flops | bytes accessed | tf_op | source)
XLA Modules:
  0.0 1317.8 jit_solution(9279652733436138874)
XLA Ops:
  0.6 0.0 copy-start
  0.6 0.7 compare_select_fusion
  1.4 2.9 broadcast_multiply_fusion.1
  4.3 0.3 subtract_convert_fusion.1
  4.6 0.1 fusion.69
  4.7 0.5 copy.95
  5.3 0.2 reshape.463
  5.5 0.5 copy.93
  6.0 0.2 reshape.462
  6.2 17.1 %copy.92 = bf16[1,32,512,384]{2,3,1,0:T(8,128)(2,1)} copy(bf16[1,32,512,384]{3,2,1,0:T(8,128)(2,1)} %param.10) | data formatting | bytes 25165824 | tf_op args[0]
  23.4 6.7 convert_reduce_fusion
  30.1 0.0 copy-start.6
  30.1 8.4 fusion.11
  38.5 0.0 copy-done.6
  38.5 14.6 %fusion.67 = f32[512,32,384]{2,0,1:T(8,128)} fusion(bf16[512,512,1]{1,0,2:T(8,128)(2,1)S(1)} %reshape.462, bf16[1,32,512,384]{2,3,1,0:T(8,128)(2,1)} %copy.92, f32[384]{0:T(512)S(1)} %copy-done.6, f32[32,512]{1,0:T(8,128)S(1)} %add_rsqrt_fusion.1, f32[32,512]{1,0:T(8,128)S(1)} %broadcast_multiply_fusion.4), kind=kOutput, calls=%fused_computation.116 | convolution fusion | flops 6473908224 | bytes 38405632 | tf_op jit(solution)/shard_map/kj,ljc->klc/dot_general | solution.py:66
  53.1 21.6 %add_convert_fusion.1 = bf16[512,32,384]{2,0,1:T(8,128)(2,1)} fusion(f32[512,32,384]{2,0,1:T(8,128)} %fusion.67, bf16[512,512,1]{1,0,2:T(8,128)(2,1)S(1)} %reshape.463, bf16[1,32,512,384]{2,3,1,0:T(8,128)(2,1)} %copy.92, f32[384]{0:T(512)S(1)} %copy-done.6, f32[32,512]{1,0:T(8,128)S(1)} %add_rsqrt_fusion.1, f32[32,512]{1,0:T(8,128)S(1)} %broadcast_multiply_fusion.4), kind=kOutput, calls=%fused_computation.23 | convolution fusion | flops 6486491136 | bytes 50988544 | tf_op jit(solution)/shard_map/kj,ljc->klc/dot_general | solution.py:67
  74.7 14.7 %copy.120 = bf16[512,32,384]{2,1,0:T(8,128)(2,1)} copy(bf16[512,32,384]{2,0,1:T(8,128)(2,1)} %add_convert_fusion.1) | data formatting | bytes 25165824 | tf_op jit(solution)/shard_map/reshape | solution.py:70
  89.4 6.5 all-to-all-start
  95.9 0.1 dynamic_slice.6
  96.0 1.2 slice_bitcast_fusion.5
  97.2 0.2 copy.100
  97.4 0.2 copy.101
  97.5 0.1 fusion.79
  97.6 272.2 %all-to-all-done = bf16[256,2,32,384]{3,2,1,0:T(8,128)(2,1)} async-done(((bf16[256,2,32,384]{3,2,1,0:T(8,128)(2,1)}), bf16[256,2,32,384]{3,2,1,0:T(8,128)(2,1)}, u32[]{:S(2)}, u32[]{:S(2)}) %all-to-all-start) | async-done | bytes 12582944 | tf_op jit(solution)/shard_map/all_to_all | solution.py:71
  369.8 11.4 copy.98
  381.2 14.3 %multiply_bitcast_fusion = f32[32,2,256,384]{2,3,1,0:T(8,128)} fusion(f32[32,256]{1,0:T(8,128)S(1)} %fusion.79, bf16[32,2,256,384]{3,2,1,0:T(8,128)(2,1)} %bitcast.186, bf16[32,256,256]{2,1,0:T(8,128)(2,1)} %param.13), kind=kOutput, calls=%fused_computation.22 | convolution fusion | flops 3227516928 | bytes 41975808 | tf_op jit(solution)/shard_map/sln,srnc->srlc/dot_general | solution.py:78
  395.5 14.9 %subtract_convert_fusion = (bf16[32,1,256,384]{2,3,1,0:T(8,128)(2,1)}, bf16[32,1,256,384]{2,3,1,0:T(8,128)(2,1)}) fusion(f32[32,2,256,384]{2,3,1,0:T(8,128)} %multiply_bitcast_fusion, f32[256,384]{0,1:T(8,128)S(1)} %copy.101, f32[256,384]{0,1:T(8,128)S(1)} %copy.100), kind=kLoop, calls=%fused_computation.56 | loop fusion | flops 25165824 | bytes 38535168 | tf_op jit(solution)/shard_map/convert.12
  410.4 10.7 convert_bitcast_fusion.1
  421.1 31.5 %copy.102 = bf16[32,2,256,384]{3,1,0,2:T(2,128)(2,1)} copy(bf16[32,2,256,384]{2,3,1,0:T(8,128)(2,1)} %convert_bitcast_fusion.1) | data formatting | bytes 25165824 | tf_op jit(solution)/shard_map/convert_element_type | solution.py:93
  452.6 5.6 all-to-all-start.1
  458.2 0.5 copy.105
  458.7 0.2 reshape.466
  458.9 0.5 copy.107
  459.5 0.2 reshape.467
  459.7 272.2 %all-to-all-done.1 = bf16[32,2,256,384]{3,1,0,2:T(2,128)(2,1)} async-done(((bf16[32,2,256,384]{3,1,0,2:T(2,128)(2,1)}), bf16[32,2,256,384]{3,1,0,2:T(2,128)(2,1)}, u32[]{:S(2)}, u32[]{:S(2)}) %all-to-all-start.1) | async-done | bytes 12582944 | tf_op jit(solution)/shard_map/all_to_all | solution.py:94
  731.9 9.5 copy.103
  741.4 6.5 copy.104
  748.0 17.1 %copy.106 = bf16[512,32,384]{0,2,1:T(8,128)(2,1)} copy(bf16[512,32,384]{2,1,0:T(8,128)(2,1)} %bitcast.189) | data formatting | bytes 25165824 | tf_op jit(solution)/shard_map/reshape | solution.py:95
  765.0 16.4 %fusion.87 = f32[32,384,512]{2,1,0:T(8,128)} fusion(bf16[512,32,384]{0,2,1:T(8,128)(2,1)} %copy.106, bf16[512,512,1]{1,0,2:T(8,128)(2,1)S(1)} %reshape.466), kind=kOutput, calls=%fused_computation.174 | convolution fusion | flops 6442450944 | bytes 38273024 | tf_op jit(solution)/shard_map/kj,klc->ljc/dot_general | solution.py:101
  781.5 28.8 %fusion.86 = (f32[32,512]{1,0:T(8,128)S(1)}, f32[32,512,384]{1,2,0:T(8,128)}) fusion(f32[32,384,512]{2,1,0:T(8,128)} %fusion.87, bf16[512,32,384]{0,2,1:T(8,128)(2,1)} %copy.106, bf16[512,512,1]{1,0,2:T(8,128)(2,1)S(1)} %reshape.467, bf16[1,32,512,384]{2,3,1,0:T(8,128)(2,1)} %copy.92), kind=kOutput, calls=%fused_computation.173 | convolution fusion | flops 6467600384 | bytes 76087296 | tf_op jit(solution)/shard_map/kj,klc->ljc/dot_general | solution.py:102
  810.3 0.0 copy-start.4
  810.3 11.6 multiply_reduce_fusion
  822.0 3.7 copy-done.2
  825.7 7.4 multiply_convert_fusion
  833.1 16.7 %copy.109 = bf16[32,512,384]{2,1,0:T(8,128)(2,1)} copy(bf16[32,512,384]{1,2,0:T(8,128)(2,1)} %multiply_convert_fusion) | data formatting | bytes 25165824 | tf_op jit(solution)/shard_map/convert_element_type | solution.py:108
  849.7 0.0 copy-done
  849.8 34.1 %fusion.15 = f32[16384,384]{1,0:T(8,128)} fusion(bf16[768,384]{1,0:T(8,128)(2,1)S(1)} %copy-done, bf16[16384,384]{1,0:T(8,128)(2,1)} %bitcast.194, bf16[384,768]{1,0:T(8,128)(2,1)S(1)} %copy-done.5), kind=kOutput, calls=%fused_computation.24 | convolution fusion | flops 19440599040 | bytes 38928384 | tf_op jit(solution)/shard_map/dot_general | solution.py:114
  883.9 24.7 %copy.110 = f32[32,512,384]{1,2,0:T(8,128)} copy(f32[32,512,384]{2,1,0:T(8,128)} %bitcast.190) | data formatting | bytes 50331648 | tf_op jit(solution)/shard_map/reshape | solution.py:114
  908.6 21.3 %fusion.19 = bf16[1,32,512,384]{2,3,1,0:T(8,128)(2,1)} fusion(f32[32,512,384]{1,2,0:T(8,128)} %get-tuple-element.53, f32[32,512,384]{1,2,0:T(8,128)} %copy.110), kind=kLoop, calls=%fused_computation.46 | loop fusion | flops 12582912 | bytes 62914560 | tf_op jit(solution)/shard_map/broadcast_in_dim | solution.py:117
  929.9 16.8 %copy.111 = bf16[1,32,512,384]{3,1,0,2:T(8,128)(2,1)} copy(bf16[1,32,512,384]{2,3,1,0:T(8,128)(2,1)} %fusion.19) | data formatting | bytes 25165824 | tf_op jit(solution)/shard_map/broadcast_in_dim | solution.py:117
  946.8 6.5 all-to-all-start.2
  953.3 137.4 %all-to-all-done.2 = bf16[1,32,512,384]{3,1,0,2:T(8,128)(2,1)} async-done(((bf16[1,32,512,384]{3,1,0,2:T(8,128)(2,1)}), bf16[1,32,512,384]{3,1,0,2:T(8,128)(2,1)}, u32[]{:S(2)}, u32[]{:S(2)}) %all-to-all-start.2) | async-done | bytes 12582944 | tf_op jit(solution)/shard_map/all_to_all | solution.py:119
  1090.7 10.2 copy.122
  1100.9 0.0 slice-start.2
  1100.9 35.1 %multiply_reduce_fusion.16 = (f32[32,128]{1,0:T(8,128)S(1)}, f32[32,128]{1,0:T(8,128)S(1)}, f32[32,128]{1,0:T(8,128)S(1)}, f32[32,128]{1,0:T(8,128)S(1)}, f32[32...) fusion(bf16[32,512,384]{2,1,0:T(8,128)(2,1)} %param.11, ...), kind=kLoop, calls=%fused_computation.101 | loop fusion | flops 102154240 | bytes 16056324 | tf_op jit(solution)/shard_map/reduce_sum | solution.py:20
  1136.4 5.2 fusion.65
  1141.7 5.3 fusion.63
  1147.0 5.3 fusion.64
  1152.3 5.3 fusion.62
  1157.6 6.0 pad_maximum_fusion
  1163.6 6.3 all-to-all-start.3
  1169.9 16.6 %copy.114 = bf16[1,32,512,384]{3,2,1,0:T(8,128)(2,1)} copy(bf16[1,32,512,384]{2,3,1,0:T(8,128)(2,1)} %fusion.19) | data formatting | bytes 25165824
  1186.5 120.3 %all-to-all-done.3 = bf16[4,32,128,384]{3,2,1,0:T(8,128)(2,1)} async-done(((bf16[4,32,128,384]{3,2,1,0:T(8,128)(2,1)}), bf16[4,32,128,384]{3,2,1,0:T(8,128)(2,1)}, u32[]{:S(2)}, u32[]{:S(2)}) %all-to-all-start.3) | async-done | bytes 12582944 | tf_op jit(solution)/shard_map/all_to_all | solution.py:131
  1306.9 10.8 copy.113
  (38 shorter events, 0.3 us)
Async XLA Ops:
  0.6 849.1 %copy-start = (bf16[768,384]{1,0:T(8,128)(2,1)S(1)}, bf16[768,384]{1,0:T(8,128)(2,1)}, u32[]{:S(2)}) copy-start(bf16[768,384]{1,0:T(8,128)(2,1)} %param.19) | copy-start | bytes 1769476
  30.1 8.4 copy-start.6
  89.4 6.5 copy-start.3
  89.4 280.3 %all-to-all-start = ((bf16[256,2,32,384]{3,2,1,0:T(8,128)(2,1)}), bf16[256,2,32,384]{3,2,1,0:T(8,128)(2,1)}, u32[]{:S(2)}, u32[]{:S(2)}) async-start(bf16[256,2,32,384]{3,2,1,0:T(8,128)(2,1)} %bitcast.187), calls=%async_computation | async-start | bytes 25165824 | tf_op jit(solution)/shard_map/all_to_all | solution.py:71
  452.6 279.3 %all-to-all-start.1 = ((bf16[32,2,256,384]{3,1,0,2:T(2,128)(2,1)}), bf16[32,2,256,384]{3,1,0,2:T(2,128)(2,1)}, u32[]{:S(2)}, u32[]{:S(2)}) async-start(bf16[32,2,256,384]{3,1,0,2:T(2,128)(2,1)} %copy.102), calls=%async_computation.1 | async-start | bytes 25165824 | tf_op jit(solution)/shard_map/all_to_all | solution.py:94
  810.3 15.4 %copy-start.2 = (f32[32,512,384]{1,2,0:T(8,128)S(1)}, f32[32,512,384]{1,2,0:T(8,128)}, u32[]{:S(2)}) copy-start(f32[32,512,384]{1,2,0:T(8,128)} %get-tuple-element.53) | copy-start | bytes 75497472
  810.3 15.4 %copy-start.4 = (f32[384]{0:T(512)S(1)}, f32[384]{0:T(512)}, u32[]{:S(2)}) copy-start(f32[384]{0:T(512)} %param.17) | copy-start | bytes 4612
  833.1 16.7 %copy-start.5 = (bf16[384,768]{1,0:T(8,128)(2,1)S(1)}, bf16[384,768]{1,0:T(8,128)(2,1)}, u32[]{:S(2)}) copy-start(bf16[384,768]{1,0:T(8,128)(2,1)} %param.18) | copy-start | bytes 1769476
  946.8 144.0 %all-to-all-start.2 = ((bf16[1,32,512,384]{3,1,0,2:T(8,128)(2,1)}), bf16[1,32,512,384]{3,1,0,2:T(8,128)(2,1)}, u32[]{:S(2)}, u32[]{:S(2)}) async-start(bf16[1,32,512,384]{3,1,0,2:T(8,128)(2,1)} %copy.111), calls=%async_computation.2 | async-start | bytes 25165824 | tf_op jit(solution)/shard_map/all_to_all | solution.py:119
  1090.7 45.7 %slice-start = ((s8[12582912]{0:T(1024)(128)(4,1)}), s8[4194304]{0:T(1024)(128)(4,1)S(1)}, s32[]{:S(2)}) async-start(s8[12582912]{0:T(1024)(128)(4,1)} %bitcast.191), calls=%async_computation.4 | async-start | bytes 8388608
  1090.7 45.7 %slice-start.1 = ((s8[12582912]{0:T(1024)(128)(4,1)}), s8[4194304]{0:T(1024)(128)(4,1)S(1)}, s32[]{:S(2)}) async-start(s8[12582912]{0:T(1024)(128)(4,1)} %bitcast.191), calls=%async_computation.5 | async-start | bytes 8388608
  1100.9 35.5 %slice-start.2 = ((s8[12582912]{0:T(1024)(128)(4,1)}), s8[4194304]{0:T(1024)(128)(4,1)S(1)}, s32[]{:S(2)}) async-start(s8[12582912]{0:T(1024)(128)(4,1)} %bitcast.191), calls=%async_computation.6 | async-start | bytes 8388608
  1163.6 143.3 %all-to-all-start.3 = ((bf16[4,32,128,384]{3,2,1,0:T(8,128)(2,1)}), bf16[4,32,128,384]{3,2,1,0:T(8,128)(2,1)}, u32[]{:S(2)}, u32[]{:S(2)}) async-start(bf16[4,32,128,384]{3,2,1,0:T(8,128)(2,1)} %pad_maximum_fusion), calls=%async_computation.3 | async-start | bytes 25165824 | tf_op jit(solution)/shard_map/all_to_all | solution.py:131
  1306.9 10.8 copy-start.1
where the time goes:
time: 1330 us; the launch traced here: 1320 us
  waiting for transfers between devices  802 us (60%)
  local copies, waits for them, and re-layouts  212 us (16%)
  matrix products  141 us (11%)
  other arithmetic  137 us (10%)
  starting transfers between devices  24.9 us (2%)
    all_to_all x1, waiting for transfers between devices, local(): lax.all_to_all(synthesis, 'lat', split_axis=2, concat_axis=0, tiled=True)  272 us
    all_to_all x1, waiting for transfers between devices, local(): lax.all_to_all(analysis, 'lat', split_axis=0, concat_axis=2, tiled=True)  272 us
    all_to_all x1, waiting for transfers between devices, local(): lax.all_to_all(predicted_field, 'member', split_axis=2, concat_axis=0, ti...  137 us
    all_to_all x1, waiting for transfers between devices, local(): lax.all_to_all(grads, 'member', split_axis=0, concat_axis=2, tiled=True)  120 us
    unnamed x22, local copies, waits for them, and re-layouts  37.5 us
    reduce_sum x1, other arithmetic, distance(): jnp.mean(jnp.square(first - second), -1, keepdims=True) + EPS_DIST  35.1 us
    dot_general x1, matrix products, local(): jnp.dot(hidden, weight_out, preferred_element_type=jnp.float32)  34.1 us
    convert_element_type x1, local copies, waits for them, and re-layouts, local(): synthesis = synthesis.astype(jnp.bfloat16)  31.5 us
  transfers between devices with their start and end apart: 4, of which 4 were waited for; matrix products, arithmetic and copies ran while one was open for 1% of the time, Pallas kernels for 0%

commit v1 on v0

--- a/solution.py
+++ b/solution.py
@@ -1,12 +1,25 @@
+import functools
 import math
 
 import jax
 import jax.numpy as jnp
 from jax import lax
+from jax.experimental import pallas as pl
+from jax.experimental.pallas import tpu as pltpu
 from jax.sharding import PartitionSpec as P
+
 
 EPS_NORM = 1e-05
 EPS_DIST = 1e-06
+LANES = 128
+BAND = 8
+PART = 64
+FINE = 16
+SPAN = 256
+EARLY = 2
+NUMBER = 8
+F32 = jnp.float32
+BF16 = jnp.bfloat16
 
 
 def layer_norm(values, scales):
@@ -16,14 +29,511 @@
     return centred * lax.rsqrt(spread + EPS_NORM) * scales
 
 
+def matmul(left, right):
+    return jnp.dot(left, right, preferred_element_type=F32)
+
+
+def params(**extra):
+    return pltpu.CompilerParams(vmem_limit_bytes=56 << 20, **extra)
+
+
+def cost(flops, bytes_accessed):
+    return pl.CostEstimate(flops=int(flops), bytes_accessed=int(bytes_accessed), transcendentals=0)
+
+
+def anywhere():
+    return pl.BlockSpec(memory_space=pl.ANY)
+
+
+def analysis_body(parts, field_ref, gain_ref, table_ref, *refs):
+    outs = refs[:parts]
+    normed, held = refs[parts:]
+    band, length, channels = field_ref.shape
+    orders = table_ref.shape[0]
+    each = orders // parts
+    pair = normed.shape[0]
+
+    def some_rows(step, carry):
+        for lane in range(pair):
+            row = step * pair + lane
+            for start in range(0, length, PART):
+                values = field_ref[row, start : start + PART, :].astype(F32)
+                normed[lane, start : start + PART, :] = layer_norm(values, gain_ref[...]).astype(
+                    BF16
+                )
+            lines = matmul(table_ref[...], normed[lane])
+            for tile in range(channels // LANES):
+                held[tile, pl.ds(pl.multiple_of(row * orders, orders), orders), :] = lines[
+                    :, tile * LANES : (tile + 1) * LANES
+                ]
+        return carry
+
+    lax.fori_loop(0, band // pair, some_rows, 0)
+    for part in range(parts):
+
+        def one_order(index, carry, part=part):
+            for tile in range(channels // LANES):
+                outs[part][index, :, tile * LANES : (tile + 1) * LANES] = held[
+                    tile, pl.ds(part * each + index, band, stride=orders), :
+                ].astype(BF16)
+            return carry
+
+        lax.fori_loop(0, each, one_order, 0, unroll=8)
+
+
+def analyse(field, gain, table, parts, first, count):
+    _, length, channels = field.shape
+    orders = table.shape[0]
+    each = orders // parts
+    return pl.pallas_call(
+        functools.partial(analysis_body, parts),
+        grid=(count // BAND,),
+        in_specs=[
+            pl.BlockSpec((BAND, length, channels), lambda i: (first // BAND + i, 0, 0)),
+            pl.BlockSpec((1, channels), lambda i: (0, 0)),
+            pl.BlockSpec((orders, length), lambda i: (0, 0)),
+        ],
+        out_specs=[pl.BlockSpec((each, BAND, channels), lambda i: (0, i, 0))] * parts,
+        out_shape=[jax.ShapeDtypeStruct((each, count, channels), BF16)] * parts,
+        scratch_shapes=[
+            pltpu.VMEM((2, length, channels), BF16),
+            pltpu.VMEM((channels // LANES, BAND * orders, LANES), F32),
+        ],
+        compiler_params=params(),
+        cost_estimate=cost(2 * count * orders * length * channels, 3 * count * length * channels),
+    )(field, gain, table)
+
+
+def spectral_body(parts, total, offsets, targets, passed, scalars, *refs):
+    pieces = len(offsets)
+    slabs = refs[: pieces * parts]
+    forward_ref, inverse_ref, filter_ref = refs[pieces * parts : pieces * parts + 3]
+    first = pieces * parts + 3 + passed
+    count = len(targets) * parts
+    outs = refs[first : first + count]
+    spectra, held = refs[first + count :]
+    slot = pl.program_id(0)
+    own = scalars[0]
+    wave = scalars[2 + slot]
+    degrees, latitudes = forward_ref.shape[1:]
+    channels = filter_ref.shape[2]
+    for piece in range(pieces):
+        for part in range(parts):
+            slab = slabs[piece * parts + part]
+            rows = slab.shape[1]
+            origin = lax.rem(own + parts - part, parts) * total + offsets[piece]
+            place = pl.ds(pl.multiple_of(origin, rows), rows)
+            for ri in range(2):
+                spectra[ri, place, :] = slab[ri]
+    order = lax.broadcasted_iota(jnp.int32, (degrees, 1), 0)
+    retain = order >= wave
+    for tile in range(channels // LANES):
+        lanes = slice(tile * LANES, (tile + 1) * LANES)
+        both = jnp.concatenate([spectra[0, :, lanes], spectra[1, :, lanes]], 1)
+        coeffs = matmul(forward_ref[0], both)
+        coeffs = jnp.where(retain, coeffs, 0.0)
+        real_part, imag_part = coeffs[:, :LANES], coeffs[:, LANES:]
+        filt_real, filt_imag = filter_ref[0, :, lanes], filter_ref[1, :, lanes]
+        filtered = jnp.concatenate(
+            [
+                (real_part * filt_real - imag_part * filt_imag).astype(BF16),
+                (real_part * filt_imag + imag_part * filt_real).astype(BF16),
+            ],
+            1,
+        )
+        profile = matmul(inverse_ref[0], filtered)
+        for ri in range(2):
+            start = pl.multiple_of((2 * slot + ri) * latitudes, latitudes)
+            held[tile, pl.ds(start, latitudes), :] = profile[:, ri * LANES : (ri + 1) * LANES]
+
+    @pl.when(slot == pl.num_programs(0) - 1)
+    def _():
+        for index, (offset, size) in enumerate(targets):
+            for part in range(parts):
+                out = outs[index * parts + part]
+                base = lax.rem(own + part, parts) * total + offset
+
+                def one_row(row, carry, out=out, base=base):
+                    for tile in range(channels // LANES):
+                        out[row, :, tile * LANES : (tile + 1) * LANES] = held[
+                            tile, pl.ds(base + row, out.shape[1], stride=latitudes), :
+                        ].astype(BF16)
+                    return carry
+
+                lax.fori_loop(0, size, one_row, 0, unroll=4)
+
+
+def spectral(scalars, pieces, forward, inverse, spec_filter, first, number, targets):
+    parts = len(pieces[0][1])
+    degrees, latitudes = forward.shape[1:]
+    channels = spec_filter.shape[2]
+    operands = []
+    in_specs = []
+    for _, slabs in pieces:
+        for slab in slabs:
+            operands.append(slab)
+            in_specs.append(pl.BlockSpec((2,) + slab.shape[1:], lambda s, *_: (s, 0, 0)))
+    operands += [forward, inverse, spec_filter]
+    in_specs += [
+        pl.BlockSpec((1, degrees, latitudes), lambda s, *_: (first + s, 0, 0)),
+        pl.BlockSpec((1, latitudes, degrees), lambda s, *_: (first + s, 0, 0)),
+        pl.BlockSpec((2, degrees, channels), lambda s, *_: (0, 0, 0)),
+    ]
+    out_shape = []
+    out_specs = []
+    aliases = {}
+    passed = 0
+    for _, size, held_slots, block, carried in targets:
+        for part in range(parts):
+            if carried is not None:
+                aliases[1 + len(operands)] = len(out_shape)
+                operands.append(carried[part])
+                in_specs.append(anywhere())
+                passed += 1
+            out_shape.append(jax.ShapeDtypeStruct((size, 2 * held_slots, channels), BF16))
+            out_specs.append(
+                pl.BlockSpec((size, 2 * number, channels), lambda s, *_, block=block: (0, block, 0))
+            )
+    outs = pl.pallas_call(
+        functools.partial(
+            spectral_body,
+            parts,
+            latitudes // parts,
+            tuple(offset for offset, _ in pieces),
+            tuple(target[:2] for target in targets),
+            passed,
+        ),
+        grid_spec=pltpu.PrefetchScalarGridSpec(
+            num_scalar_prefetch=1,
+            grid=(number,),
+            in_specs=in_specs,
+            out_specs=out_specs,
+            scratch_shapes=[
+                pltpu.VMEM((2, latitudes, channels), BF16),
+                pltpu.VMEM((channels // LANES, 2 * number * latitudes, LANES), F32),
+            ],
+        ),
+        out_shape=out_shape,
+        input_output_aliases=aliases,
+        compiler_params=params(),
+        cost_estimate=cost(
+            8 * number * degrees * latitudes * channels,
+            8 * number * latitudes * channels + 4 * number * degrees * latitudes,
+        ),
+    )(scalars, *operands)
+    return [outs[index * parts : (index + 1) * parts] for index in range(len(targets))]
+
+
+def finish_body(parts, members, continued, scalars, *refs):
+    slabs = refs[:parts]
+    field_ref, table_ref, gain_ref, into_ref, from_ref = refs[parts : parts + 5]
+    first = parts + 5 + (1 if continued else 0)
+    predicted_ref = refs[first]
+    sends = refs[first + 1 : first + 1 + members]
+    after_ref, normed_ref = refs[first + 1 + members :]
+    length = field_ref.shape[1]
+    lines = jnp.concatenate([slab[0] for slab in slabs], 0)
+    after_ref[...] = matmul(table_ref[...], lines) + field_ref[0].astype(F32)
+    for start in range(0, length, PART):
+        normed_ref[start : start + PART, :] = layer_norm(
+            after_ref[start : start + PART, :], gain_ref[...]
+        ).astype(BF16)
+    step = 256 if length % 256 == 0 else length
+    for start in range(0, length, step):
+        rows = slice(start, start + step)
+        hidden = jax.nn.gelu(matmul(normed_ref[rows, :], into_ref[...])).astype(BF16)
+        predicted_ref[0, rows, :] = (after_ref[rows, :] + matmul(hidden, from_ref[...])).astype(
+            BF16
+        )
+    share = pl.num_programs(0) // members
+    for part in range(members):
+
+        @pl.when(pl.program_id(0) // share == part)
+        def _(part=part):
+            sends[part][0] = predicted_ref[0]
+
+
+def finish(scalars, slabs, field, table, gain, into, out_of, carried, offset, members):
+    parts = len(slabs)
+    size, _, channels = slabs[0].shape
+    _, length = field.shape[:2]
+    share = size // members
+
+    def position(r, sc):
+        return lax.rem(sc[1] + r // share, members) * share + lax.rem(r, share)
+
+    def whole(r, sc):
+        return (offset + position(r, sc), 0, 0)
+
+    def fixed(r, sc):
+        return (0, 0)
+
+    in_specs = [
+        pl.BlockSpec((1,) + slab.shape[1:], lambda r, sc: (position(r, sc), 0, 0))
+        for slab in slabs
+    ]
+    in_specs += [
+        pl.BlockSpec((1, length, channels), whole),
+        pl.BlockSpec(table.shape, fixed),
+        pl.BlockSpec(gain.shape, fixed),
+        pl.BlockSpec(into.shape, fixed),
+        pl.BlockSpec(out_of.shape, fixed),
+    ]
+    aliases = {}
+    if carried is not None:
+        in_specs.append(anywhere())
+        aliases = {1 + parts + 5: 0}
+    out_specs = [pl.BlockSpec((1, length, channels), whole)]
+    out_shape = [jax.ShapeDtypeStruct(field.shape, BF16)]
+    for part in range(members):
+        out_specs.append(
+            pl.BlockSpec(
+                (1, length, channels),
+                lambda r, sc, part=part: (jnp.clip(r - part * share, 0, share - 1), 0, 0),
+            )
+        )
+        out_shape.append(jax.ShapeDtypeStruct((share, length, channels), BF16))
+    hidden = into.shape[1]
+    return pl.pallas_call(
+        functools.partial(finish_body, parts, members, carried is not None),
+        grid_spec=pltpu.PrefetchScalarGridSpec(
+            num_scalar_prefetch=1,
+            grid=(size,),
+            in_specs=in_specs,
+            out_specs=out_specs,
+            scratch_shapes=[
+                pltpu.VMEM((length, channels), F32),
+                pltpu.VMEM((length, channels), BF16),
+            ],
+        ),
+        out_shape=out_shape,
+        input_output_aliases=aliases,
+        compiler_params=params(),
+        cost_estimate=cost(
+            2 * size * length * channels * (table.shape[1] + 2 * hidden),
+            8 * size * length * channels,
+        ),
+    )(scalars, *slabs, field, table, gain, into, out_of, *([] if carried is None else [carried]))
+
+
+def score_body(members, continued, scalars, *refs):
+    fields = refs[:members]
+    target_ref = refs[members]
+    outs = refs[members + 1 + continued :]
+    length, channels = target_ref.shape[1:]
+
+    def one_part(index, carry):
+        place = pl.ds(pl.multiple_of(index * FINE, FINE), FINE)
+        values = [field[0, place, :].astype(F32) for field in fields]
+        target = target_ref[0, place, :].astype(F32)
+
+        def pull(first, second, scale):
+            apart = first - second
+            mean_square = jnp.sum(apart * apart, -1, keepdims=True) * (1.0 / channels)
+            return apart * (lax.rsqrt(mean_square + EPS_DIST) * scale)
+
+        slopes = [pull(value, target, 1.0) for value in values]
+        for one in range(members):
+            for other in range(one + 1, members):
+                term = pull(values[one], values[other], 1.0 / (members - 1))
+                slopes[one] = slopes[one] - term
+                slopes[other] = slopes[other] + term
+        for one in range(members):
+            outs[one][0, place, :] = slopes[one].astype(BF16)
+        return carry
+
+    lax.fori_loop(0, length // FINE, one_part, 0, unroll=2)
+
+
+def score(scalars, fields, observed, carried, offset):
+    members = len(fields)
+    share, length, channels = fields[0].shape
+
+    def block(r, j, sc):
+        return (r, j, 0)
+
+    def whole(r, j, sc):
+        return (offset + sc[1] * share + r, j, 0)
+
+    span = SPAN if length % SPAN == 0 else length
+    spec = pl.BlockSpec((1, span, channels), block)
+    placed = pl.BlockSpec((1, span, channels), whole)
+    piece = jax.ShapeDtypeStruct((share, length, channels), BF16)
+    out_specs = [placed] + [spec] * (members - 1)
+    out_shape = [jax.ShapeDtypeStruct(observed.shape, BF16)] + [piece] * (members - 1)
+    continued = carried is not None
+    return pl.pallas_call(
+        functools.partial(score_body, members, continued),
+        grid_spec=pltpu.PrefetchScalarGridSpec(
+            num_scalar_prefetch=1,
+            grid=(share, length // span),
+            in_specs=[spec] * members + [placed] + [anywhere()] * continued,
+            out_specs=out_specs,
+        ),
+        out_shape=out_shape,
+        input_output_aliases={members + 2: 0} if continued else {},
+        compiler_params=params(),
+        cost_estimate=cost(100 * share * length * channels, 18 * share * length * channels),
+    )(scalars, *fields, observed, *([carried] if continued else []))
+
+
+def shift(array, axis, step):
+    size = lax.axis_size(axis)
+    return lax.ppermute(array, axis, [(i, (i + step) % size) for i in range(size)])
+
+
+def place(whole, pieces):
+    for piece, start in pieces:
+        whole = lax.dynamic_update_slice_in_dim(whole, piece, start, 0)
+    return whole
+
+
+def angles_of(numbers, columns, length):
+    phases = numbers * columns % length
+    return phases.astype(F32) * (2.0 * math.pi / length)
+
+
+def chunk_sizes(rows, unit):
+    units = rows // unit
+    if units < 6:
+        return (unit,) * units
+    middle = units - 4
+    sizes = [1, 1] + [2] * (middle // 2) + [1] * (middle % 2) + [1, 1]
+    return tuple(unit * size for size in sizes)
+
+
+def pipelined(
+    field,
+    observed,
+    wave_of_slot,
+    leg_forward,
+    leg_inverse,
+    spec_filter,
+    gain_first,
+    gain_second,
+    weight_in,
+    weight_out,
+):
+    rows, length, channels = field.shape
+    slots = leg_forward.shape[0]
+    parts = lax.axis_size("lat")
+    members = lax.axis_size("member")
+    own = lax.axis_index("lat")
+    own_member = lax.axis_index("member")
+    number = NUMBER
+    groups = slots // number
+    chunks = chunk_sizes(rows, members)
+    gain_first = gain_first.reshape(1, channels)
+    gain_second = gain_second.reshape(1, channels)
+    scalars = jnp.stack([own, own_member]).astype(jnp.int32)
+
+    waves = wave_of_slot.reshape(parts, groups, number)
+    steps = jnp.arange(parts, dtype=jnp.int32)
+    columns = jnp.arange(length, dtype=jnp.int32)
+    outgoing = jnp.take(waves, (own + steps) % parts, axis=0).transpose(1, 0, 2)
+    angles = angles_of(outgoing[..., None, None], columns, length)
+    turn = jnp.arange(2, dtype=jnp.int32)[:, None]
+    tables = jnp.where(turn == 0, jnp.cos(angles), -jnp.sin(angles)) * (1.0 / length)
+    tables = tables.astype(BF16).reshape(groups, parts * number * 2, length)
+    incoming = jnp.take(wave_of_slot.reshape(parts, slots), (own - steps) % parts, axis=0)
+    incoming = jnp.repeat(incoming.reshape(-1), 2)
+    angles = angles_of(incoming[None, :], columns[:, None], length)
+    weights = jnp.where(incoming == 0, 1.0, 2.0).astype(F32)[None, :]
+    even = (jnp.arange(incoming.shape[0]) % 2 == 0)[None, :]
+    back_table = (weights * jnp.where(even, jnp.cos(angles), -jnp.sin(angles))).astype(BF16)
+    local_waves = lax.dynamic_slice_in_dim(wave_of_slot, own * slots, slots)
+
+    def spread(slabs):
+        return [slabs[0]] + [shift(slabs[part], "lat", part) for part in range(1, parts)]
+
+    received = []
+    for group in range(groups):
+        halves = 2 if group == 0 else 1
+        pieces = []
+        for half in range(halves):
+            count = rows // halves
+            slabs = analyse(field, gain_first, tables[group], parts, half * count, count)
+            pieces.append((half * count, spread(slabs)))
+        received.append(pieces)
+    starts = [sum(chunks[:index]) for index in range(len(chunks))]
+    early = [None] * EARLY
+    profiles = [None] * len(chunks)
+    for group in range(groups):
+        numbers = jnp.concatenate(
+            [scalars, local_waves[group * number : (group + 1) * number]]
+        )
+        last = group == groups - 1
+        targets = []
+        for index in range(len(chunks)):
+            place_of = (starts[index], chunks[index])
+            if index >= EARLY:
+                targets.append(place_of + (slots, group, profiles[index]))
+            elif last:
+                targets.append(place_of + (number, 0, None))
+            else:
+                targets.append(place_of + (slots - number, group, early[index]))
+        profiles = spectral(
+            numbers,
+            received[group],
+            leg_forward,
+            leg_inverse,
+            spec_filter,
+            group * number,
+            number,
+            targets,
+        )
+        if not last:
+            early = profiles[:EARLY]
+        if group == groups - 2:
+            arrived = []
+            for index in range(EARLY):
+                arrived.append(spread(early[index]))
+
+    predicted = None
+    slope = None
+    offset = 0
+    placed = []
+    for index, size in enumerate(chunks):
+        slabs = spread(profiles[index])
+        if index < EARLY:
+            slabs = [slab for both in zip(arrived[index], slabs) for slab in both]
+        predicted, *sends = finish(
+            scalars,
+            slabs,
+            field,
+            back_table,
+            gain_second,
+            weight_in,
+            weight_out,
+            predicted,
+            offset,
+            members,
+        )
+        fields = [sends[0]] + [
+            shift(sends[part], "member", part) for part in range(1, members)
+        ]
+        slope, *grads = score(scalars, fields, observed, slope, offset)
+        share = size // members
+        pieces = []
+        for part in range(1, members):
+            back = shift(grads[part - 1], "member", members - part)
+            pieces.append((back, offset + (own_member + part) % members * share))
+        placed.append(pieces)
+        offset += size
+        if index >= 2:
+            slope = place(slope, placed[index - 2])
+    for pieces in placed[max(len(chunks) - 2, 0) :]:
+        slope = place(slope, pieces)
+    return predicted[None], slope[None]
+
+
 def distance(first, second):
     return jnp.sqrt(jnp.mean(jnp.square(first - second), -1, keepdims=True) + EPS_DIST)
 
 
 def dft_tables(numbers, length):
     columns = jnp.arange(length, dtype=jnp.int32)
-    phases = numbers[:, None] * columns[None, :] % length
-    angles = phases.astype(jnp.float32) * (2.0 * math.pi / length)
+    angles = angles_of(numbers[:, None], columns[None, :], length)
     return (jnp.cos(angles), jnp.sin(angles))
 
 
@@ -58,6 +568,31 @@
     waves_all = wave_of_slot.shape[0]
     slots = leg_forward.shape[0]
     degrees = leg_forward.shape[1]
+    parts = lax.axis_size("lat")
+    members = lax.axis_size("member")
+    if (
+        lat_rows % 16 == 0
+        and lat_rows % members == 0
+        and slots % NUMBER == 0
+        and slots >= 2 * NUMBER
+        and lat_rows >= 2 * members
+        and channels % LANES == 0
+        and length % PART == 0
+        and degrees % 16 == 0
+        and slots * parts == waves_all
+    ):
+        return pipelined(
+            ensemble_starting_fields[0],
+            observed,
+            wave_of_slot,
+            leg_forward,
+            leg_inverse,
+            spec_filter,
+            gain_first,
+            gain_second,
+            weight_in,
+            weight_out,
+        )
     values = ensemble_starting_fields[0].astype(jnp.float32)
     normed = layer_norm(values, gain_first).astype(jnp.bfloat16)
     cosines, sines = dft_tables(wave_of_slot, length)
@@ -98,11 +633,11 @@
         2 * waves_all, length
     )
     inv_high, inv_low = split_table(inv_table)
-    spectral = jnp.einsum("kj,klc->ljc", inv_high, returned, preferred_element_type=jnp.float32)
-    spectral = spectral + jnp.einsum(
+    spectral_part = jnp.einsum("kj,klc->ljc", inv_high, returned, preferred_element_type=F32)
+    spectral_part = spectral_part + jnp.einsum(
         "kj,klc->ljc", inv_low, returned, preferred_element_type=jnp.float32
     )
-    harmonic_damped_field = values + spectral
+    harmonic_damped_field = values + spectral_part
     normed_two = (
         layer_norm(harmonic_damped_field, gain_second)
         .astype(jnp.bfloat16)
@@ -115,7 +650,6 @@
         lat_rows, length, channels
     )
     predicted_field = (harmonic_damped_field + feedforward_result).astype(jnp.bfloat16)[None]
-    members = lax.axis_size("member")
     gathered_fields = lax.all_to_all(
         predicted_field, "member", split_axis=2, concat_axis=0, tiled=True
     )

time: 1330 us -> 946 us (0.71)
  waiting for transfers between devices: 802 us -> 224 us
  starting transfers between devices: 24.9 us -> 395 us
  Pallas kernels: 0 us -> 266 us
  local copies, waits for them, and re-layouts: 212 us -> 38.5 us
  matrix products: 141 us -> 0 us
  other arithmetic: 137 us -> 10.4 us
    all_to_all x4 -> x0, waiting for transfers between devices: 802 us -> none  [the longest x1 272 us: local(): lax.all_to_all(synthesis, 'lat', split_axis=2, concat_axis=0, tiled=True)]
    ppermute x0 -> x127, starting transfers between devices: none -> 395 us  [shift(): lax.ppermute(array, axis, [(i, (i + step) % size) for i in range(size)])]
    pallas_call x0 -> x21, Pallas kernels: none -> 266 us  [the longest x6 84.3 us: finish(): pl.pallas_call(functools.partial(finish_body, parts, members, carried is...]
    ppermute x0 -> x127, waiting for transfers between devices: none -> 224 us  [shift(): lax.ppermute(array, axis, [(i, (i + step) % size) for i in range(size)])]
    dot_general x7 -> x0, matrix products: 141 us -> none  [the longest x1 34.1 us: local(): jnp.dot(hidden, weight_out, preferred_element_type=jnp.float32)]
    reduce_sum x4 -> x0, other arithmetic: 61.8 us -> none  [the longest x1 35.1 us: distance(): jnp.mean(jnp.square(first - second), -1, keepdims=True) + EPS_DIST]
    reshape x3 -> x5, local copies, waits for them, and re-layouts: 56.5 us -> 2.83 us  [the longest x1 1.26 us: pipelined(): gain_first = gain_first.reshape(1, channels)]
    convert_element_type x10 -> x0, local copies, waits for them, and re-layouts: 51.2 us -> none  [the longest x1 31.5 us: local(): synthesis = synthesis.astype(jnp.bfloat16)]
  transfers between devices with their start and end apart: 4 -> 127, of which waited for: 4 -> 30; matrix products, arithmetic and copies ran while one was open for 1% -> 3% of each run, Pallas kernels for 0% -> 26%
where the time goes in v1:
time: 946 us; the launch traced here: 937 us
  starting transfers between devices  395 us (42%)
  Pallas kernels  266 us (28%)
  waiting for transfers between devices  224 us (24%)
  local copies, waits for them, and re-layouts  38.5 us (4%)
  other arithmetic  10.4 us (1%)
    ppermute x127, starting transfers between devices, shift(): lax.ppermute(array, axis, [(i, (i + step) % size) for i in range(size)])  395 us
    ppermute x127, waiting for transfers between devices, shift(): lax.ppermute(array, axis, [(i, (i + step) % size) for i in range(size)])  224 us
    pallas_call x6, Pallas kernels, finish(): pl.pallas_call(functools.partial(finish_body, parts, members, carried is...  84.3 us
    pallas_call x5, Pallas kernels, analyse(): pl.pallas_call(functools.partial(analysis_body, parts), grid=(count // BA...  79.8 us
    pallas_call x4, Pallas kernels, spectral(): pl.pallas_call(functools.partial(spectral_body, parts, latitudes // parts...  63.4 us
    pallas_call x6, Pallas kernels, score(): pl.pallas_call(functools.partial(score_body, members, continued), grid_sp...  38.7 us
    dynamic_update_slice x18, local copies, waits for them, and re-layouts, place(): whole = lax.dynamic_update_slice_in_dim(whole, piece, start, 0)  20.2 us
  transfers between devices with their start and end apart: 127, of which 30 were waited for; matrix products, arithmetic and copies ran while one was open for 3% of the time, Pallas kernels for 26%

profile of v1, /device:TPU:0, one launch (start us, length us, event | category | flops | bytes accessed | tf_op | source)
XLA Modules:
  0.0 936.7 jit_solution(4582547530510535007)
XLA Ops:
  7.5 11.0 %shard_map.116 = (bf16[16,16,384]{2,1,0:T(8,128)(2,1)}, bf16[16,16,384]{2,1,0:T(8,128)(2,1)}, bf16[16,16,384]{2,1,0:T(8,128)(2,1)}, bf16[16,16,384]{2,1,0:T(8,12...) custom-call(bf16[32,512,384]{2,1,0:T(8,128)(2,1)} %bitcast.29, ...), custom_call_target="tpu_custom_call" | custom-call | flops 805306368 | bytes 9437184 | tf_op jit(solution)/shard_map/pallas_call | solution.py:88
  30.4 11.1 %shard_map.117 = (bf16[16,16,384]{2,1,0:T(8,128)(2,1)}, bf16[16,16,384]{2,1,0:T(8,128)(2,1)}, bf16[16,16,384]{2,1,0:T(8,128)(2,1)}, bf16[16,16,384]{2,1,0:T(8,12...) custom-call(bf16[32,512,384]{2,1,0:T(8,128)(2,1)} %bitcast.30, ...), custom_call_target="tpu_custom_call" | custom-call | flops 805306368 | bytes 9437184 | tf_op jit(solution)/shard_map/pallas_call | solution.py:88
  41.6 4.0 collective-permute-done.23.refs_3_
  45.8 8.3 collective-permute-start.29
  56.9 19.2 %shard_map.113 = (bf16[16,32,384]{2,1,0:T(8,128)(2,1)}, bf16[16,32,384]{2,1,0:T(8,128)(2,1)}, bf16[16,32,384]{2,1,0:T(8,128)(2,1)}, bf16[16,32,384]{2,1,0:T(8,12...) custom-call(bf16[32,512,384]{2,1,0:T(8,128)(2,1)} %bitcast.31, ...), custom_call_target="tpu_custom_call" | custom-call | flops 1610612736 | bytes 18874368 | tf_op jit(solution)/shard_map/pallas_call | solution.py:88
  77.5 3.6 collective-permute-start.31
  84.6 19.3 %shard_map.114 = (bf16[16,32,384]{2,1,0:T(8,128)(2,1)}, bf16[16,32,384]{2,1,0:T(8,128)(2,1)}, bf16[16,32,384]{2,1,0:T(8,128)(2,1)}, bf16[16,32,384]{2,1,0:T(8,12...) custom-call(bf16[32,512,384]{2,1,0:T(8,128)(2,1)} %bitcast.32, ...), custom_call_target="tpu_custom_call" | custom-call | flops 1610612736 | bytes 18874368 | tf_op jit(solution)/shard_map/pallas_call | solution.py:88
  113.2 19.3 %shard_map.115 = (bf16[16,32,384]{2,1,0:T(8,128)(2,1)}, bf16[16,32,384]{2,1,0:T(8,128)(2,1)}, bf16[16,32,384]{2,1,0:T(8,128)(2,1)}, bf16[16,32,384]{2,1,0:T(8,12...) custom-call(bf16[32,512,384]{2,1,0:T(8,128)(2,1)} %bitcast.33, ...), custom_call_target="tpu_custom_call" | custom-call | flops 1610612736 | bytes 18874368 | tf_op jit(solution)/shard_map/pallas_call | solution.py:88
  136.6 23.3 %collective-permute-done.9.refs_3_ = bf16[16,32,384]{2,1,0:T(8,128)(2,1)S(1)} collective-permute-done((bf16[16,32,384]{2,1,0:T(8,128)(2,1)}, bf16[16,32,384]{2,1,0:T(8,128)(2,1)S(1)}, u32[]{:S(2)}, u32[]{:S(2)}) %collective-permute-start.9) | collective-permute-done | bytes 393248 | tf_op jit(solution)/shard_map/ppermute | solution.py:382
  160.1 16.0 %collective-permute-start.15 = (bf16[16,32,384]{2,1,0:T(8,128)(2,1)}, bf16[16,32,384]{2,1,0:T(8,128)(2,1)}, u32[]{:S(2)}, u32[]{:S(2)}) collective-permute-start(bf16[16,32,384]{2,1,0:T(8,128)(2,1)} %get-tuple-element.306), channel_id=1, source_target_pairs={{0,2},{1,3},{2,4},{3,5},{4,6},{5,7},{6,0},{7,1},{8,10},{9,11},{10,... | collective-permute-start | bytes 1179656 | tf_op jit(solution)/shard_map/ppermute | solution.py:382
  176.1 8.1 collective-permute-start.16
  187.2 22.6 %collective-permute-start.18 = (bf16[16,32,384]{2,1,0:T(8,128)(2,1)}, bf16[16,32,384]{2,1,0:T(8,128)(2,1)}, u32[]{:S(2)}, u32[]{:S(2)}) collective-permute-start(bf16[16,32,384]{2,1,0:T(8,128)(2,1)} %get-tuple-element.309), channel_id=1, source_target_pairs={{0,5},{1,6},{2,7},{3,0},{4,1},{5,2},{6,3},{7,4},{8,13},{9,14},{10,... | collective-permute-start | bytes 1179656 | tf_op jit(solution)/shard_map/ppermute | solution.py:382
  209.8 3.2 collective-permute-start.19
  214.4 13.1 %collective-permute-done.16.refs_3_ = bf16[16,32,384]{2,1,0:T(8,128)(2,1)} collective-permute-done((bf16[16,32,384]{2,1,0:T(8,128)(2,1)}, bf16[16,32,384]{2,1,0:T(8,128)(2,1)}, u32[]{:S(2)}, u32[]{:S(2)}) %collective-permute-start.16) | collective-permute-done | bytes 393248 | tf_op jit(solution)/shard_map/ppermute | solution.py:382
  227.5 24.1 %collective-permute-start.2 = (bf16[16,32,384]{2,1,0:T(8,128)(2,1)}, bf16[16,32,384]{2,1,0:T(8,128)(2,1)S(1)}, u32[]{:S(2)}, u32[]{:S(2)}) collective-permute-start(bf16[16,32,384]{2,1,0:T(8,128)(2,1)} %get-tuple-element.291), channel_id=1, source_target_pairs={{0,3},{1,4},{2,5},{3,6},{4,7},{5,0},{6,1},{7,2},{8,11},{9,12},{10,... | collective-permute-start | bytes 1179656 | tf_op jit(solution)/shard_map/ppermute | solution.py:382
  251.6 26.2 %collective-permute-start.5 = (bf16[16,32,384]{2,1,0:T(8,128)(2,1)}, bf16[16,32,384]{2,1,0:T(8,128)(2,1)S(1)}, u32[]{:S(2)}, u32[]{:S(2)}) collective-permute-start(bf16[16,32,384]{2,1,0:T(8,128)(2,1)} %get-tuple-element.294), channel_id=1, source_target_pairs={{0,6},{1,7},{2,0},{3,1},{4,2},{5,3},{6,4},{7,5},{8,14},{9,15},{10,... | collective-permute-start | bytes 1179656 | tf_op jit(solution)/shard_map/ppermute | solution.py:382
  277.8 15.7 %shard_map.118 = (bf16[4,48,384]{2,1,0:T(8,128)(2,1)}, bf16[4,48,384]{2,1,0:T(8,128)(2,1)}, bf16[4,48,384]{2,1,0:T(8,128)(2,1)}, bf16[4,48,384]{2,1,0:T(8,128)(2...) custom-call(s32[10]{0:T(128)} %get-tuple-element.574.scalars, ...), custom_call_target="tpu_custom_call" | custom-call | flops 1610612736 | bytes 8388608 | tf_op jit(solution)/shard_map/pallas_call | solution.py:197
  293.5 15.9 %shard_map.119 = (bf16[4,48,384]{2,1,0:T(8,128)(2,1)}, bf16[4,48,384]{2,1,0:T(8,128)(2,1)}, bf16[4,48,384]{2,1,0:T(8,128)(2,1)}, bf16[4,48,384]{2,1,0:T(8,128)(2...) custom-call(s32[10]{0:T(128)} %get-tuple-element.582.scalars, ...), custom_call_target="tpu_custom_call", output_to_operand_aliasing={{0}: (12, {}), {1}: (13, {}), {2}: (14, {}), {3}: (15, {}),... | custom-call | flops 1610612736 | bytes 8388608 | tf_op jit(solution)/shard_map/pallas_call | solution.py:197
  309.5 16.2 %shard_map.120 = (bf16[4,48,384]{2,1,0:T(8,128)(2,1)}, bf16[4,48,384]{2,1,0:T(8,128)(2,1)}, bf16[4,48,384]{2,1,0:T(8,128)(2,1)}, bf16[4,48,384]{2,1,0:T(8,128)(2...) custom-call(s32[10]{0:T(128)} %get-tuple-element.583.scalars, ...), custom_call_target="tpu_custom_call", output_to_operand_aliasing={{0}: (12, {}), {1}: (13, {}), {2}: (14, {}), {3}: (15, {}),... | custom-call | flops 1610612736 | bytes 8388608 | tf_op jit(solution)/shard_map/pallas_call | solution.py:197
  327.2 15.6 %shard_map.121 = (bf16[4,16,384]{2,1,0:T(8,128)(2,1)}, bf16[4,16,384]{2,1,0:T(8,128)(2,1)}, bf16[4,16,384]{2,1,0:T(8,128)(2,1)}, bf16[4,16,384]{2,1,0:T(8,128)(2...) custom-call(s32[10]{0:T(128)} %get-tuple-element.584.scalars, ...), custom_call_target="tpu_custom_call", output_to_operand_aliasing={{16}: (12, {}), {17}: (13, {}), {18}: (14, {}), {19}: (15, ... | custom-call | flops 1610612736 | bytes 8388608 | tf_op jit(solution)/shard_map/pallas_call | solution.py:197
  343.6 3.4 collective-permute-start.70
  359.1 5.2 collective-permute-done.80.refs_5_
  377.0 5.3 collective-permute-done.67.refs_6_
  384.0 5.3 collective-permute-start.79
  391.3 4.0 collective-permute-start.83
  399.3 8.0 collective-permute-start.36
  412.8 9.5 %collective-permute-start.89 = (bf16[4,48,384]{2,1,0:T(8,128)(2,1)S(1)}, bf16[4,48,384]{2,1,0:T(8,128)(2,1)S(1)}, u32[]{:S(2)}, u32[]{:S(2)}) collective-permute-start(bf16[4,48,384]{2,1,0:T(8,128)(2,1)S(1)} %copy-done.20), channel_id=1, source_target_pairs={{0,7},{1,0},{2,1},{3,2},{4,3},{5,4},{6,5},{7,6},{8,15},{9,8},{10,9... | collective-permute-start | bytes 442376 | tf_op jit(solution)/shard_map/ppermute | solution.py:382
  425.5 8.2 collective-permute-start.39
  433.7 3.5 collective-permute-start.40
  439.4 12.4 %collective-permute-start.49 = (bf16[8,64,384]{2,1,0:T(8,128)(2,1)}, bf16[8,64,384]{2,1,0:T(8,128)(2,1)S(1)}, u32[]{:S(2)}, u32[]{:S(2)}) collective-permute-start(bf16[8,64,384]{2,1,0:T(8,128)(2,1)} %get-tuple-element.473), channel_id=1, source_target_pairs={{0,1},{1,2},{2,3},{3,4},{4,5},{5,6},{6,7},{7,0},{8,9},{9,10},{10,1... | collective-permute-start | bytes 1179656 | tf_op jit(solution)/shard_map/ppermute | solution.py:382
  454.3 29.6 %collective-permute-start.57 = (bf16[8,64,384]{2,1,0:T(8,128)(2,1)}, bf16[8,64,384]{2,1,0:T(8,128)(2,1)S(1)}, u32[]{:S(2)}, u32[]{:S(2)}) collective-permute-start(bf16[8,64,384]{2,1,0:T(8,128)(2,1)} %get-tuple-element.482), channel_id=1, source_target_pairs={{0,2},{1,3},{2,4},{3,5},{4,6},{5,7},{6,0},{7,1},{8,10},{9,11},{10,... | collective-permute-start | bytes 1179656 | tf_op jit(solution)/shard_map/ppermute | solution.py:382
  485.2 5.3 multiply_convert_fusion.refs_17_.refs_9_
  490.5 6.5 collective-permute-done.44.refs_3_
  497.7 15.8 %collective-permute-start.58 = (bf16[8,64,384]{2,1,0:T(8,128)(2,1)}, bf16[8,64,384]{2,1,0:T(8,128)(2,1)S(1)}, u32[]{:S(2)}, u32[]{:S(2)}) collective-permute-start(bf16[8,64,384]{2,1,0:T(8,128)(2,1)} %get-tuple-element.483), channel_id=1, source_target_pairs={{0,3},{1,4},{2,5},{3,6},{4,7},{5,0},{6,1},{7,2},{8,11},{9,12},{10,... | collective-permute-start | bytes 1179656 | tf_op jit(solution)/shard_map/ppermute | solution.py:382
  513.6 5.6 collective-permute-start.61
  519.5 11.6 %shard_map.122 = (bf16[32,512,384]{2,1,0:T(8,128)(2,1)}, bf16[1,512,384]{2,1,0:T(8,128)(2,1)}, bf16[1,512,384]{2,1,0:T(8,128)(2,1)}, bf16[1,512,384]{2,1,0:T(8,128)(2,1)}, bf16[1,512,384]{2,1,0:T(8,128)(2,1)}) custom-call(s32[2]{0:T(128)} %pad_add_fusion.scalars, bf16[4,48,384]{2,1,0:T(8,128)(2,1)} %get-tuple-element.504.refs_0_, ...), custom_call_target="tpu_custom_call" | custom-call | flops 3221225472 | bytes 6291456 | tf_op jit(solution)/shard_map/pallas_call | solution.py:297
  531.2 11.8 %shard_map.123 = (bf16[32,512,384]{2,1,0:T(8,128)(2,1)}, bf16[1,512,384]{2,1,0:T(8,128)(2,1)}, bf16[1,512,384]{2,1,0:T(8,128)(2,1)}, bf16[1,512,384]{2,1,0:T(8,128)(2,1)}, bf16[1,512,384]{2,1,0:T(8,128)(2,1)}) custom-call(s32[2]{0:T(128)} %pad_add_fusion.scalars, bf16[4,48,384]{2,1,0:T(8,128)(2,1)} %get-tuple-element.488.refs_0_, ...), custom_call_target="tpu_custom_call", output_to_operand_aliasing={{0}: (22, {})} | custom-call | flops 3221225472 | bytes 6291456 | tf_op jit(solution)/shard_map/pallas_call | solution.py:297
  543.1 16.0 %collective-permute-start.51 = (bf16[8,64,384]{2,1,0:T(8,128)(2,1)S(1)}, bf16[8,64,384]{2,1,0:T(8,128)(2,1)S(1)}, u32[]{:S(2)}, u32[]{:S(2)}) collective-permute-start(bf16[8,64,384]{2,1,0:T(8,128)(2,1)S(1)} %copy-done), channel_id=1, source_target_pairs={{0,3},{1,4},{2,5},{3,6},{4,7},{5,0},{6,1},{7,2},{8,11},{9,12},{10,... | collective-permute-start | bytes 1179656 | tf_op jit(solution)/shard_map/ppermute | solution.py:382
  559.3 26.0 %collective-permute-start.54 = (bf16[8,64,384]{2,1,0:T(8,128)(2,1)S(1)}, bf16[8,64,384]{2,1,0:T(8,128)(2,1)S(1)}, u32[]{:S(2)}, u32[]{:S(2)}) collective-permute-start(bf16[8,64,384]{2,1,0:T(8,128)(2,1)S(1)} %copy-done.3), channel_id=1, source_target_pairs={{0,6},{1,7},{2,0},{3,1},{4,2},{5,3},{6,4},{7,5},{8,14},{9,15},{10,... | collective-permute-start | bytes 1179656 | tf_op jit(solution)/shard_map/ppermute | solution.py:382
  586.1 19.3 %shard_map.124 = (bf16[32,512,384]{2,1,0:T(8,128)(2,1)}, bf16[2,512,384]{2,1,0:T(8,128)(2,1)}, bf16[2,512,384]{2,1,0:T(8,128)(2,1)}, bf16[2,512,384]{2,1,0:T(8,128)(2,1)}, bf16[2,512,384]{2,1,0:T(8,128)(2,1)}) custom-call(s32[2]{0:T(128)} %pad_add_fusion.scalars, bf16[8,64,384]{2,1,0:T(8,128)(2,1)} %get-tuple-element.480.refs_0_, ...), custom_call_target="tpu_custom_call", output_to_operand_aliasing={{0}: (14, {})} | custom-call | flops 6442450944 | bytes 12582912 | tf_op jit(solution)/shard_map/pallas_call | solution.py:297
  607.7 12.7 %collective-permute-start.47 = (bf16[4,64,384]{2,1,0:T(8,128)(2,1)S(1)}, bf16[4,64,384]{2,1,0:T(8,128)(2,1)S(1)}, u32[]{:S(2)}, u32[]{:S(2)}) collective-permute-start(bf16[4,64,384]{2,1,0:T(8,128)(2,1)S(1)} %copy-done.7), channel_id=1, source_target_pairs={{0,6},{1,7},{2,0},{3,1},{4,2},{5,3},{6,4},{7,5},{8,14},{9,15},{10,... | collective-permute-start | bytes 589832 | tf_op jit(solution)/shard_map/ppermute | solution.py:382
  620.4 9.3 collective-permute-start.48
  631.3 19.3 %shard_map.125 = (bf16[32,512,384]{2,1,0:T(8,128)(2,1)}, bf16[2,512,384]{2,1,0:T(8,128)(2,1)}, bf16[2,512,384]{2,1,0:T(8,128)(2,1)}, bf16[2,512,384]{2,1,0:T(8,128)(2,1)}, bf16[2,512,384]{2,1,0:T(8,128)(2,1)}) custom-call(s32[2]{0:T(128)} %pad_add_fusion.scalars, bf16[8,64,384]{2,1,0:T(8,128)(2,1)} %get-tuple-element.472.refs_0_, ...), custom_call_target="tpu_custom_call", output_to_operand_aliasing={{0}: (14, {})} | custom-call | flops 6442450944 | bytes 12582912 | tf_op jit(solution)/shard_map/pallas_call | solution.py:297
  655.2 11.2 %shard_map.126 = (bf16[32,512,384]{2,1,0:T(8,128)(2,1)}, bf16[1,512,384]{2,1,0:T(8,128)(2,1)}, bf16[1,512,384]{2,1,0:T(8,128)(2,1)}, bf16[1,512,384]{2,1,0:T(8,128)(2,1)}, bf16[1,512,384]{2,1,0:T(8,128)(2,1)}) custom-call(s32[2]{0:T(128)} %pad_add_fusion.scalars, bf16[4,64,384]{2,1,0:T(8,128)(2,1)} %get-tuple-element.464.refs_0_, ...), custom_call_target="tpu_custom_call", output_to_operand_aliasing={{0}: (14, {})} | custom-call | flops 3221225472 | bytes 6291456 | tf_op jit(solution)/shard_map/pallas_call | solution.py:297
  668.9 11.2 %shard_map.127 = (bf16[32,512,384]{2,1,0:T(8,128)(2,1)}, bf16[1,512,384]{2,1,0:T(8,128)(2,1)}, bf16[1,512,384]{2,1,0:T(8,128)(2,1)}, bf16[1,512,384]{2,1,0:T(8,128)(2,1)}, bf16[1,512,384]{2,1,0:T(8,128)(2,1)}) custom-call(s32[2]{0:T(128)} %pad_add_fusion.scalars, bf16[4,64,384]{2,1,0:T(8,128)(2,1)} %get-tuple-element.456.refs_0_, ...), custom_call_target="tpu_custom_call", output_to_operand_aliasing={{0}: (14, {})} | custom-call | flops 3221225472 | bytes 6291456 | tf_op jit(solution)/shard_map/pallas_call | solution.py:297
  683.8 5.7 collective-permute-start.96
  689.6 3.8 collective-permute-done.91.refs_1_
  695.5 6.3 collective-permute-done.94.refs_1_
  702.5 5.4 shard_map.128
  711.7 38.1 %collective-permute-done.109 = bf16[1,512,384]{2,1,0:T(8,128)(2,1)S(1)} collective-permute-done((bf16[1,512,384]{2,1,0:T(8,128)(2,1)}, bf16[1,512,384]{2,1,0:T(8,128)(2,1)S(1)}, u32[]{:S(2)}, u32[]{:S(2)}) %collective-permute-start.109) | collective-permute-done | bytes 393248 | tf_op jit(solution)/shard_map/ppermute | solution.py:382
  751.1 6.1 collective-permute-start.99
  757.2 5.6 shard_map.129
  765.8 8.3 shard_map.130
  774.1 22.5 %collective-permute-done.111 = bf16[1,512,384]{2,1,0:T(8,128)(2,1)S(1)} collective-permute-done((bf16[1,512,384]{2,1,0:T(8,128)(2,1)S(1)}, bf16[1,512,384]{2,1,0:T(8,128)(2,1)S(1)}, u32[]{:S(2)}, u32[]{:S(2)}) %collective-permute-start.111) | collective-permute-done | bytes 393248 | tf_op jit(solution)/shard_map/ppermute | solution.py:382
  796.6 8.0 collective-permute-done.112
  815.4 8.3 shard_map.131
  823.6 29.8 %collective-permute-done.113 = bf16[1,512,384]{2,1,0:T(8,128)(2,1)} collective-permute-done((bf16[1,512,384]{2,1,0:T(8,128)(2,1)}, bf16[1,512,384]{2,1,0:T(8,128)(2,1)}, u32[]{:S(2)}, u32[]{:S(2)}) %collective-permute-start.113) | collective-permute-done | bytes 393248 | tf_op jit(solution)/shard_map/ppermute | solution.py:382
  858.2 5.6 shard_map.132
  870.4 23.6 %collective-permute-done.92.refs_2_ = bf16[1,512,384]{2,1,0:T(8,128)(2,1)S(1)} collective-permute-done((bf16[1,512,384]{2,1,0:T(8,128)(2,1)S(1)}, bf16[1,512,384]{2,1,0:T(8,128)(2,1)S(1)}, u32[]{:S(2)}, u32[]{:S(2)}) %collective-permute-start.92) | collective-permute-done | bytes 393248 | tf_op jit(solution)/shard_map/ppermute | solution.py:382
  894.0 5.5 collective-permute-start.121
  900.3 5.6 shard_map.133
  913.8 5.6 collective-permute-done.122
  920.9 6.1 collective-permute-done.124
  927.8 7.2 collective-permute-done.125
  (551 shorter events, 156.0 us)
Async XLA Ops:
  27.9 48.2 %collective-permute-start.26 = (bf16[16,16,384]{2,1,0:T(8,128)(2,1)}, bf16[16,16,384]{2,1,0:T(8,128)(2,1)S(1)}, u32[]{:S(2)}, u32[]{:S(2)}) collective-permute-start(bf16[16,16,384]{2,1,0:T(8,128)(2,1)} %get-tuple-element.318), channel_id=1, source_target_pairs={{0,6},{1,7},{2,0},{3,1},{4,2},{5,3},{6,4},{7,5},{8,14},{9,15},{10,... | collective-permute-start | bytes 589832 | tf_op jit(solution)/shard_map/ppermute | solution.py:382
  41.6 35.9 %collective-permute-start.27 = (bf16[16,16,384]{2,1,0:T(8,128)(2,1)S(1)}, bf16[16,16,384]{2,1,0:T(8,128)(2,1)}, u32[]{:S(2)}, u32[]{:S(2)}) collective-permute-start(bf16[16,16,384]{2,1,0:T(8,128)(2,1)S(1)} %copy-done.144), channel_id=1, source_target_pairs={{0,7},{1,0},{2,1},{3,2},{4,3},{5,4},{6,5},{7,6},{8,15},{9,8},{10,9... | collective-permute-start | bytes 589832 | tf_op jit(solution)/shard_map/ppermute | solution.py:382
  45.7 35.4 %collective-permute-start.28 = (bf16[16,16,384]{2,1,0:T(8,128)(2,1)}, bf16[16,16,384]{2,1,0:T(8,128)(2,1)}, u32[]{:S(2)}, u32[]{:S(2)}) collective-permute-start(bf16[16,16,384]{2,1,0:T(8,128)(2,1)} %get-tuple-element.321), channel_id=1, source_target_pairs={{0,1},{1,2},{2,3},{3,4},{4,5},{5,6},{6,7},{7,0},{8,9},{9,10},{10,1... | collective-permute-start | bytes 589832 | tf_op jit(solution)/shard_map/ppermute | solution.py:382
  45.8 36.6 %collective-permute-start.29 = (bf16[16,16,384]{2,1,0:T(8,128)(2,1)}, bf16[16,16,384]{2,1,0:T(8,128)(2,1)}, u32[]{:S(2)}, u32[]{:S(2)}) collective-permute-start(bf16[16,16,384]{2,1,0:T(8,128)(2,1)} %get-tuple-element.322), channel_id=1, source_target_pairs={{0,2},{1,3},{2,4},{3,5},{4,6},{5,7},{6,0},{7,1},{8,10},{9,11},{10,... | collective-permute-start | bytes 589832 | tf_op jit(solution)/shard_map/ppermute | solution.py:382
  76.8 34.3 %collective-permute-start = (bf16[16,32,384]{2,1,0:T(8,128)(2,1)}, bf16[16,32,384]{2,1,0:T(8,128)(2,1)S(1)}, u32[]{:S(2)}, u32[]{:S(2)}) collective-permute-start(bf16[16,32,384]{2,1,0:T(8,128)(2,1)} %get-tuple-element.289), channel_id=1, source_target_pairs={{0,1},{1,2},{2,3},{3,4},{4,5},{5,6},{6,7},{7,0},{8,9},{9,10},{10,1... | collective-permute-start | bytes 1179656 | tf_op jit(solution)/shard_map/ppermute | solution.py:382
  108.7 51.1 %collective-permute-start.9 = (bf16[16,32,384]{2,1,0:T(8,128)(2,1)}, bf16[16,32,384]{2,1,0:T(8,128)(2,1)S(1)}, u32[]{:S(2)}, u32[]{:S(2)}) collective-permute-start(bf16[16,32,384]{2,1,0:T(8,128)(2,1)} %get-tuple-element.299), channel_id=1, source_target_pairs={{0,3},{1,4},{2,5},{3,6},{4,7},{5,0},{6,1},{7,2},{8,11},{9,12},{10,... | collective-permute-start | bytes 1179656 | tf_op jit(solution)/shard_map/ppermute | solution.py:382
  111.1 48.9 %collective-permute-start.10 = (bf16[16,32,384]{2,1,0:T(8,128)(2,1)}, bf16[16,32,384]{2,1,0:T(8,128)(2,1)S(1)}, u32[]{:S(2)}, u32[]{:S(2)}) collective-permute-start(bf16[16,32,384]{2,1,0:T(8,128)(2,1)} %get-tuple-element.300), channel_id=1, source_target_pairs={{0,4},{1,5},{2,6},{3,7},{4,0},{5,1},{6,2},{7,3},{8,12},{9,13},{10,... | collective-permute-start | bytes 1179656 | tf_op jit(solution)/shard_map/ppermute | solution.py:382
  132.5 43.6 %collective-permute-start.11 = (bf16[16,32,384]{2,1,0:T(8,128)(2,1)}, bf16[16,32,384]{2,1,0:T(8,128)(2,1)S(1)}, u32[]{:S(2)}, u32[]{:S(2)}) collective-permute-start(bf16[16,32,384]{2,1,0:T(8,128)(2,1)} %get-tuple-element.301), channel_id=1, source_target_pairs={{0,5},{1,6},{2,7},{3,0},{4,1},{5,2},{6,3},{7,4},{8,13},{9,14},{10,... | collective-permute-start | bytes 1179656 | tf_op jit(solution)/shard_map/ppermute | solution.py:382
  134.5 49.7 %collective-permute-start.12 = (bf16[16,32,384]{2,1,0:T(8,128)(2,1)}, bf16[16,32,384]{2,1,0:T(8,128)(2,1)S(1)}, u32[]{:S(2)}, u32[]{:S(2)}) collective-permute-start(bf16[16,32,384]{2,1,0:T(8,128)(2,1)} %get-tuple-element.302), channel_id=1, source_target_pairs={{0,6},{1,7},{2,0},{3,1},{4,2},{5,3},{6,4},{7,5},{8,14},{9,15},{10,... | collective-permute-start | bytes 1179656 | tf_op jit(solution)/shard_map/ppermute | solution.py:382
  136.6 50.6 %collective-permute-start.13 = (bf16[16,32,384]{2,1,0:T(8,128)(2,1)}, bf16[16,32,384]{2,1,0:T(8,128)(2,1)}, u32[]{:S(2)}, u32[]{:S(2)}) collective-permute-start(bf16[16,32,384]{2,1,0:T(8,128)(2,1)} %get-tuple-element.303), channel_id=1, source_target_pairs={{0,7},{1,0},{2,1},{3,2},{4,3},{5,4},{6,5},{7,6},{8,15},{9,8},{10,9... | collective-permute-start | bytes 1179656 | tf_op jit(solution)/shard_map/ppermute | solution.py:382
  159.9 49.9 %collective-permute-start.14 = (bf16[16,32,384]{2,1,0:T(8,128)(2,1)}, bf16[16,32,384]{2,1,0:T(8,128)(2,1)}, u32[]{:S(2)}, u32[]{:S(2)}) collective-permute-start(bf16[16,32,384]{2,1,0:T(8,128)(2,1)} %get-tuple-element.305), channel_id=1, source_target_pairs={{0,1},{1,2},{2,3},{3,4},{4,5},{5,6},{6,7},{7,0},{8,9},{9,10},{10,1... | collective-permute-start | bytes 1179656 | tf_op jit(solution)/shard_map/ppermute | solution.py:382
  160.1 53.0 %collective-permute-start.15 = (bf16[16,32,384]{2,1,0:T(8,128)(2,1)}, bf16[16,32,384]{2,1,0:T(8,128)(2,1)}, u32[]{:S(2)}, u32[]{:S(2)}) collective-permute-start(bf16[16,32,384]{2,1,0:T(8,128)(2,1)} %get-tuple-element.306), channel_id=1, source_target_pairs={{0,2},{1,3},{2,4},{3,5},{4,6},{5,7},{6,0},{7,1},{8,10},{9,11},{10,... | collective-permute-start | bytes 1179656 | tf_op jit(solution)/shard_map/ppermute | solution.py:382
  176.1 51.3 %collective-permute-start.16 = (bf16[16,32,384]{2,1,0:T(8,128)(2,1)}, bf16[16,32,384]{2,1,0:T(8,128)(2,1)}, u32[]{:S(2)}, u32[]{:S(2)}) collective-permute-start(bf16[16,32,384]{2,1,0:T(8,128)(2,1)} %get-tuple-element.307), channel_id=1, source_target_pairs={{0,3},{1,4},{2,5},{3,6},{4,7},{5,0},{6,1},{7,2},{8,11},{9,12},{10,... | collective-permute-start | bytes 1179656 | tf_op jit(solution)/shard_map/ppermute | solution.py:382
  184.2 67.3 %collective-permute-start.17 = (bf16[16,32,384]{2,1,0:T(8,128)(2,1)}, bf16[16,32,384]{2,1,0:T(8,128)(2,1)}, u32[]{:S(2)}, u32[]{:S(2)}) collective-permute-start(bf16[16,32,384]{2,1,0:T(8,128)(2,1)} %get-tuple-element.308), channel_id=1, source_target_pairs={{0,4},{1,5},{2,6},{3,7},{4,0},{5,1},{6,2},{7,3},{8,12},{9,13},{10,... | collective-permute-start | bytes 1179656 | tf_op jit(solution)/shard_map/ppermute | solution.py:382
  187.2 64.3 %collective-permute-start.18 = (bf16[16,32,384]{2,1,0:T(8,128)(2,1)}, bf16[16,32,384]{2,1,0:T(8,128)(2,1)}, u32[]{:S(2)}, u32[]{:S(2)}) collective-permute-start(bf16[16,32,384]{2,1,0:T(8,128)(2,1)} %get-tuple-element.309), channel_id=1, source_target_pairs={{0,5},{1,6},{2,7},{3,0},{4,1},{5,2},{6,3},{7,4},{8,13},{9,14},{10,... | collective-permute-start | bytes 1179656 | tf_op jit(solution)/shard_map/ppermute | solution.py:382
  209.8 41.8 %collective-permute-start.19 = (bf16[16,32,384]{2,1,0:T(8,128)(2,1)}, bf16[16,32,384]{2,1,0:T(8,128)(2,1)}, u32[]{:S(2)}, u32[]{:S(2)}) collective-permute-start(bf16[16,32,384]{2,1,0:T(8,128)(2,1)} %get-tuple-element.310), channel_id=1, source_target_pairs={{0,6},{1,7},{2,0},{3,1},{4,2},{5,3},{6,4},{7,5},{8,14},{9,15},{10,... | collective-permute-start | bytes 1179656 | tf_op jit(solution)/shard_map/ppermute | solution.py:382
  213.0 64.8 %collective-permute-start.20 = (bf16[16,32,384]{2,1,0:T(8,128)(2,1)}, bf16[16,32,384]{2,1,0:T(8,128)(2,1)}, u32[]{:S(2)}, u32[]{:S(2)}) collective-permute-start(bf16[16,32,384]{2,1,0:T(8,128)(2,1)} %get-tuple-element.311), channel_id=1, source_target_pairs={{0,7},{1,0},{2,1},{3,2},{4,3},{5,4},{6,5},{7,6},{8,15},{9,8},{10,9... | collective-permute-start | bytes 1179656 | tf_op jit(solution)/shard_map/ppermute | solution.py:382
  227.5 98.4 %collective-permute-start.2 = (bf16[16,32,384]{2,1,0:T(8,128)(2,1)}, bf16[16,32,384]{2,1,0:T(8,128)(2,1)S(1)}, u32[]{:S(2)}, u32[]{:S(2)}) collective-permute-start(bf16[16,32,384]{2,1,0:T(8,128)(2,1)} %get-tuple-element.291), channel_id=1, source_target_pairs={{0,3},{1,4},{2,5},{3,6},{4,7},{5,0},{6,1},{7,2},{8,11},{9,12},{10,... | collective-permute-start | bytes 1179656 | tf_op jit(solution)/shard_map/ppermute | solution.py:382
  251.6 74.3 %collective-permute-start.3 = (bf16[16,32,384]{2,1,0:T(8,128)(2,1)}, bf16[16,32,384]{2,1,0:T(8,128)(2,1)S(1)}, u32[]{:S(2)}, u32[]{:S(2)}) collective-permute-start(bf16[16,32,384]{2,1,0:T(8,128)(2,1)} %get-tuple-element.292), channel_id=1, source_target_pairs={{0,4},{1,5},{2,6},{3,7},{4,0},{5,1},{6,2},{7,3},{8,12},{9,13},{10,... | collective-permute-start | bytes 1179656 | tf_op jit(solution)/shard_map/ppermute | solution.py:382
  251.6 74.3 %collective-permute-start.4 = (bf16[16,32,384]{2,1,0:T(8,128)(2,1)}, bf16[16,32,384]{2,1,0:T(8,128)(2,1)S(1)}, u32[]{:S(2)}, u32[]{:S(2)}) collective-permute-start(bf16[16,32,384]{2,1,0:T(8,128)(2,1)} %get-tuple-element.293), channel_id=1, source_target_pairs={{0,5},{1,6},{2,7},{3,0},{4,1},{5,2},{6,3},{7,4},{8,13},{9,14},{10,... | collective-permute-start | bytes 1179656 | tf_op jit(solution)/shard_map/ppermute | solution.py:382
  251.6 74.3 %collective-permute-start.5 = (bf16[16,32,384]{2,1,0:T(8,128)(2,1)}, bf16[16,32,384]{2,1,0:T(8,128)(2,1)S(1)}, u32[]{:S(2)}, u32[]{:S(2)}) collective-permute-start(bf16[16,32,384]{2,1,0:T(8,128)(2,1)} %get-tuple-element.294), channel_id=1, source_target_pairs={{0,6},{1,7},{2,0},{3,1},{4,2},{5,3},{6,4},{7,5},{8,14},{9,15},{10,... | collective-permute-start | bytes 1179656 | tf_op jit(solution)/shard_map/ppermute | solution.py:382
  277.8 48.1 %collective-permute-start.6 = (bf16[16,32,384]{2,1,0:T(8,128)(2,1)}, bf16[16,32,384]{2,1,0:T(8,128)(2,1)S(1)}, u32[]{:S(2)}, u32[]{:S(2)}) collective-permute-start(bf16[16,32,384]{2,1,0:T(8,128)(2,1)} %get-tuple-element.295), channel_id=1, source_target_pairs={{0,7},{1,0},{2,1},{3,2},{4,3},{5,4},{6,5},{7,6},{8,15},{9,8},{10,9... | collective-permute-start | bytes 1179656 | tf_op jit(solution)/shard_map/ppermute | solution.py:382
  397.3 36.4 %collective-permute-start.35 = (bf16[4,64,384]{2,1,0:T(8,128)(2,1)}, bf16[4,64,384]{2,1,0:T(8,128)(2,1)S(1)}, u32[]{:S(2)}, u32[]{:S(2)}) collective-permute-start(bf16[4,64,384]{2,1,0:T(8,128)(2,1)} %get-tuple-element.457), channel_id=1, source_target_pairs={{0,1},{1,2},{2,3},{3,4},{4,5},{5,6},{6,7},{7,0},{8,9},{9,10},{10,1... | collective-permute-start | bytes 589832 | tf_op jit(solution)/shard_map/ppermute | solution.py:382
  399.3 37.9 %collective-permute-start.36 = (bf16[4,64,384]{2,1,0:T(8,128)(2,1)}, bf16[4,64,384]{2,1,0:T(8,128)(2,1)S(1)}, u32[]{:S(2)}, u32[]{:S(2)}) collective-permute-start(bf16[4,64,384]{2,1,0:T(8,128)(2,1)} %get-tuple-element.458), channel_id=1, source_target_pairs={{0,2},{1,3},{2,4},{3,5},{4,6},{5,7},{6,0},{7,1},{8,10},{9,11},{10,... | collective-permute-start | bytes 589832 | tf_op jit(solution)/shard_map/ppermute | solution.py:382
  437.8 47.3 %collective-permute-start.43 = (bf16[4,64,384]{2,1,0:T(8,128)(2,1)}, bf16[4,64,384]{2,1,0:T(8,128)(2,1)S(1)}, u32[]{:S(2)}, u32[]{:S(2)}) collective-permute-start(bf16[4,64,384]{2,1,0:T(8,128)(2,1)} %get-tuple-element.466), channel_id=1, source_target_pairs={{0,2},{1,3},{2,4},{3,5},{4,6},{5,7},{6,0},{7,1},{8,10},{9,11},{10,... | collective-permute-start | bytes 589832 | tf_op jit(solution)/shard_map/ppermute | solution.py:382
  439.4 74.1 %collective-permute-start.49 = (bf16[8,64,384]{2,1,0:T(8,128)(2,1)}, bf16[8,64,384]{2,1,0:T(8,128)(2,1)S(1)}, u32[]{:S(2)}, u32[]{:S(2)}) collective-permute-start(bf16[8,64,384]{2,1,0:T(8,128)(2,1)} %get-tuple-element.473), channel_id=1, source_target_pairs={{0,1},{1,2},{2,3},{3,4},{4,5},{5,6},{6,7},{7,0},{8,9},{9,10},{10,1... | collective-permute-start | bytes 1179656 | tf_op jit(solution)/shard_map/ppermute | solution.py:382
  451.8 61.7 %collective-permute-start.50 = (bf16[8,64,384]{2,1,0:T(8,128)(2,1)}, bf16[8,64,384]{2,1,0:T(8,128)(2,1)S(1)}, u32[]{:S(2)}, u32[]{:S(2)}) collective-permute-start(bf16[8,64,384]{2,1,0:T(8,128)(2,1)} %get-tuple-element.474), channel_id=1, source_target_pairs={{0,2},{1,3},{2,4},{3,5},{4,6},{5,7},{6,0},{7,1},{8,10},{9,11},{10,... | collective-permute-start | bytes 1179656 | tf_op jit(solution)/shard_map/ppermute | solution.py:382
  453.0 60.6 %collective-permute-start.56 = (bf16[8,64,384]{2,1,0:T(8,128)(2,1)}, bf16[8,64,384]{2,1,0:T(8,128)(2,1)S(1)}, u32[]{:S(2)}, u32[]{:S(2)}) collective-permute-start(bf16[8,64,384]{2,1,0:T(8,128)(2,1)} %get-tuple-element.481), channel_id=1, source_target_pairs={{0,1},{1,2},{2,3},{3,4},{4,5},{5,6},{6,7},{7,0},{8,9},{9,10},{10,1... | collective-permute-start | bytes 1179656 | tf_op jit(solution)/shard_map/ppermute | solution.py:382
  454.3 65.0 %collective-permute-start.57 = (bf16[8,64,384]{2,1,0:T(8,128)(2,1)}, bf16[8,64,384]{2,1,0:T(8,128)(2,1)S(1)}, u32[]{:S(2)}, u32[]{:S(2)}) collective-permute-start(bf16[8,64,384]{2,1,0:T(8,128)(2,1)} %get-tuple-element.482), channel_id=1, source_target_pairs={{0,2},{1,3},{2,4},{3,5},{4,6},{5,7},{6,0},{7,1},{8,10},{9,11},{10,... | collective-permute-start | bytes 1179656 | tf_op jit(solution)/shard_map/ppermute | solution.py:382
  497.7 45.4 %collective-permute-start.58 = (bf16[8,64,384]{2,1,0:T(8,128)(2,1)}, bf16[8,64,384]{2,1,0:T(8,128)(2,1)S(1)}, u32[]{:S(2)}, u32[]{:S(2)}) collective-permute-start(bf16[8,64,384]{2,1,0:T(8,128)(2,1)} %get-tuple-element.483), channel_id=1, source_target_pairs={{0,3},{1,4},{2,5},{3,6},{4,7},{5,0},{6,1},{7,2},{8,11},{9,12},{10,... | collective-permute-start | bytes 1179656 | tf_op jit(solution)/shard_map/ppermute | solution.py:382
  513.5 45.6 %collective-permute-start.59 = (bf16[8,64,384]{2,1,0:T(8,128)(2,1)}, bf16[8,64,384]{2,1,0:T(8,128)(2,1)S(1)}, u32[]{:S(2)}, u32[]{:S(2)}) collective-permute-start(bf16[8,64,384]{2,1,0:T(8,128)(2,1)} %get-tuple-element.484), channel_id=1, source_target_pairs={{0,4},{1,5},{2,6},{3,7},{4,0},{5,1},{6,2},{7,3},{8,12},{9,13},{10,... | collective-permute-start | bytes 1179656 | tf_op jit(solution)/shard_map/ppermute | solution.py:382
  513.5 45.7 %collective-permute-start.60 = (bf16[8,64,384]{2,1,0:T(8,128)(2,1)}, bf16[8,64,384]{2,1,0:T(8,128)(2,1)S(1)}, u32[]{:S(2)}, u32[]{:S(2)}) collective-permute-start(bf16[8,64,384]{2,1,0:T(8,128)(2,1)} %get-tuple-element.485), channel_id=1, source_target_pairs={{0,5},{1,6},{2,7},{3,0},{4,1},{5,2},{6,3},{7,4},{8,13},{9,14},{10,... | collective-permute-start | bytes 1179656 | tf_op jit(solution)/shard_map/ppermute | solution.py:382
  513.6 45.7 %collective-permute-start.61 = (bf16[8,64,384]{2,1,0:T(8,128)(2,1)}, bf16[8,64,384]{2,1,0:T(8,128)(2,1)S(1)}, u32[]{:S(2)}, u32[]{:S(2)}) collective-permute-start(bf16[8,64,384]{2,1,0:T(8,128)(2,1)} %get-tuple-element.486), channel_id=1, source_target_pairs={{0,6},{1,7},{2,0},{3,1},{4,2},{5,3},{6,4},{7,5},{8,14},{9,15},{10,... | collective-permute-start | bytes 1179656 | tf_op jit(solution)/shard_map/ppermute | solution.py:382
  519.2 66.1 %collective-permute-start.62 = (bf16[8,64,384]{2,1,0:T(8,128)(2,1)}, bf16[8,64,384]{2,1,0:T(8,128)(2,1)S(1)}, u32[]{:S(2)}, u32[]{:S(2)}) collective-permute-start(bf16[8,64,384]{2,1,0:T(8,128)(2,1)} %get-tuple-element.487), channel_id=1, source_target_pairs={{0,7},{1,0},{2,1},{3,2},{4,3},{5,4},{6,5},{7,6},{8,15},{9,8},{10,9... | collective-permute-start | bytes 1179656 | tf_op jit(solution)/shard_map/ppermute | solution.py:382
  543.1 62.3 %collective-permute-start.51 = (bf16[8,64,384]{2,1,0:T(8,128)(2,1)S(1)}, bf16[8,64,384]{2,1,0:T(8,128)(2,1)S(1)}, u32[]{:S(2)}, u32[]{:S(2)}) collective-permute-start(bf16[8,64,384]{2,1,0:T(8,128)(2,1)S(1)} %copy-done), channel_id=1, source_target_pairs={{0,3},{1,4},{2,5},{3,6},{4,7},{5,0},{6,1},{7,2},{8,11},{9,12},{10,... | collective-permute-start | bytes 1179656 | tf_op jit(solution)/shard_map/ppermute | solution.py:382
  559.1 47.3 %collective-permute-start.52 = (bf16[8,64,384]{2,1,0:T(8,128)(2,1)S(1)}, bf16[8,64,384]{2,1,0:T(8,128)(2,1)S(1)}, u32[]{:S(2)}, u32[]{:S(2)}) collective-permute-start(bf16[8,64,384]{2,1,0:T(8,128)(2,1)S(1)} %copy-done.1), channel_id=1, source_target_pairs={{0,4},{1,5},{2,6},{3,7},{4,0},{5,1},{6,2},{7,3},{8,12},{9,13},{10,... | collective-permute-start | bytes 1179656 | tf_op jit(solution)/shard_map/ppermute | solution.py:382
  559.2 48.4 %collective-permute-start.53 = (bf16[8,64,384]{2,1,0:T(8,128)(2,1)S(1)}, bf16[8,64,384]{2,1,0:T(8,128)(2,1)S(1)}, u32[]{:S(2)}, u32[]{:S(2)}) collective-permute-start(bf16[8,64,384]{2,1,0:T(8,128)(2,1)S(1)} %copy-done.2), channel_id=1, source_target_pairs={{0,5},{1,6},{2,7},{3,0},{4,1},{5,2},{6,3},{7,4},{8,13},{9,14},{10,... | collective-permute-start | bytes 1179656 | tf_op jit(solution)/shard_map/ppermute | solution.py:382
  559.3 61.1 %collective-permute-start.54 = (bf16[8,64,384]{2,1,0:T(8,128)(2,1)S(1)}, bf16[8,64,384]{2,1,0:T(8,128)(2,1)S(1)}, u32[]{:S(2)}, u32[]{:S(2)}) collective-permute-start(bf16[8,64,384]{2,1,0:T(8,128)(2,1)S(1)} %copy-done.3), channel_id=1, source_target_pairs={{0,6},{1,7},{2,0},{3,1},{4,2},{5,3},{6,4},{7,5},{8,14},{9,15},{10,... | collective-permute-start | bytes 1179656 | tf_op jit(solution)/shard_map/ppermute | solution.py:382
  585.4 44.3 %collective-permute-start.55 = (bf16[8,64,384]{2,1,0:T(8,128)(2,1)S(1)}, bf16[8,64,384]{2,1,0:T(8,128)(2,1)S(1)}, u32[]{:S(2)}, u32[]{:S(2)}) collective-permute-start(bf16[8,64,384]{2,1,0:T(8,128)(2,1)S(1)} %copy-done.4), channel_id=1, source_target_pairs={{0,7},{1,0},{2,1},{3,2},{4,3},{5,4},{6,5},{7,6},{8,15},{9,8},{10,9... | collective-permute-start | bytes 1179656 | tf_op jit(solution)/shard_map/ppermute | solution.py:382
  605.4 45.1 %collective-permute-start.45 = (bf16[4,64,384]{2,1,0:T(8,128)(2,1)S(1)}, bf16[4,64,384]{2,1,0:T(8,128)(2,1)S(1)}, u32[]{:S(2)}, u32[]{:S(2)}) collective-permute-start(bf16[4,64,384]{2,1,0:T(8,128)(2,1)S(1)} %copy-done.5), channel_id=1, source_target_pairs={{0,4},{1,5},{2,6},{3,7},{4,0},{5,1},{6,2},{7,3},{8,12},{9,13},{10,... | collective-permute-start | bytes 589832 | tf_op jit(solution)/shard_map/ppermute | solution.py:382
  606.4 45.8 %collective-permute-start.46 = (bf16[4,64,384]{2,1,0:T(8,128)(2,1)S(1)}, bf16[4,64,384]{2,1,0:T(8,128)(2,1)S(1)}, u32[]{:S(2)}, u32[]{:S(2)}) collective-permute-start(bf16[4,64,384]{2,1,0:T(8,128)(2,1)S(1)} %copy-done.6), channel_id=1, source_target_pairs={{0,5},{1,6},{2,7},{3,0},{4,1},{5,2},{6,3},{7,4},{8,13},{9,14},{10,... | collective-permute-start | bytes 589832 | tf_op jit(solution)/shard_map/ppermute | solution.py:382
  607.7 46.0 %collective-permute-start.47 = (bf16[4,64,384]{2,1,0:T(8,128)(2,1)S(1)}, bf16[4,64,384]{2,1,0:T(8,128)(2,1)S(1)}, u32[]{:S(2)}, u32[]{:S(2)}) collective-permute-start(bf16[4,64,384]{2,1,0:T(8,128)(2,1)S(1)} %copy-done.7), channel_id=1, source_target_pairs={{0,6},{1,7},{2,0},{3,1},{4,2},{5,3},{6,4},{7,5},{8,14},{9,15},{10,... | collective-permute-start | bytes 589832 | tf_op jit(solution)/shard_map/ppermute | solution.py:382
  620.4 34.1 %collective-permute-start.48 = (bf16[4,64,384]{2,1,0:T(8,128)(2,1)S(1)}, bf16[4,64,384]{2,1,0:T(8,128)(2,1)S(1)}, u32[]{:S(2)}, u32[]{:S(2)}) collective-permute-start(bf16[4,64,384]{2,1,0:T(8,128)(2,1)S(1)} %copy-done.8), channel_id=1, source_target_pairs={{0,7},{1,0},{2,1},{3,2},{4,3},{5,4},{6,5},{7,6},{8,15},{9,8},{10,9... | collective-permute-start | bytes 589832 | tf_op jit(solution)/shard_map/ppermute | solution.py:382
  629.7 36.7 %collective-permute-start.103 = (bf16[1,512,384]{2,1,0:T(8,128)(2,1)S(1)}, bf16[1,512,384]{2,1,0:T(8,128)(2,1)S(1)}, u32[]{:S(2)}, u32[]{:S(2)}) collective-permute-start(bf16[1,512,384]{2,1,0:T(8,128)(2,1)S(1)} %copy-done.133), channel_id=1, source_target_pairs={{0,8},{8,16},{16,24},{24,0},{1,9},{9,17},{17,25},{25,1},{2,10},{10... | collective-permute-start | bytes 1179656 | tf_op jit(solution)/shard_map/ppermute | solution.py:382
  689.6 61.5 %collective-permute-start.100 = (bf16[2,512,384]{2,1,0:T(8,128)(2,1)}, bf16[2,512,384]{2,1,0:T(8,128)(2,1)S(1)}, u32[]{:S(2)}, u32[]{:S(2)}) collective-permute-start(bf16[2,512,384]{2,1,0:T(8,128)(2,1)} %get-tuple-element.539), channel_id=1, source_target_pairs={{0,8},{8,16},{16,24},{24,0},{1,9},{9,17},{17,25},{25,1},{2,10},{10... | collective-permute-start | bytes 2359304 | tf_op jit(solution)/shard_map/ppermute | solution.py:382
  694.1 68.7 %collective-permute-start.101 = (bf16[2,512,384]{2,1,0:T(8,128)(2,1)}, bf16[2,512,384]{2,1,0:T(8,128)(2,1)S(1)}, u32[]{:S(2)}, u32[]{:S(2)}) collective-permute-start(bf16[2,512,384]{2,1,0:T(8,128)(2,1)} %get-tuple-element.540), channel_id=1, source_target_pairs={{0,16},{8,24},{16,0},{24,8},{1,17},{9,25},{17,1},{25,9},{2,18},{10... | collective-permute-start | bytes 2359304 | tf_op jit(solution)/shard_map/ppermute | solution.py:382
  702.5 60.4 %collective-permute-start.102 = (bf16[2,512,384]{2,1,0:T(8,128)(2,1)S(1)}, bf16[2,512,384]{2,1,0:T(8,128)(2,1)S(1)}, u32[]{:S(2)}, u32[]{:S(2)}) collective-permute-start(bf16[2,512,384]{2,1,0:T(8,128)(2,1)S(1)} %copy-done.124), channel_id=1, source_target_pairs={{0,24},{8,0},{16,8},{24,16},{1,25},{9,1},{17,9},{25,17},{2,26},{10... | collective-permute-start | bytes 2359304 | tf_op jit(solution)/shard_map/ppermute | solution.py:382
  710.2 39.5 %collective-permute-start.109 = (bf16[1,512,384]{2,1,0:T(8,128)(2,1)}, bf16[1,512,384]{2,1,0:T(8,128)(2,1)S(1)}, u32[]{:S(2)}, u32[]{:S(2)}) collective-permute-start(bf16[1,512,384]{2,1,0:T(8,128)(2,1)} %get-tuple-element.553), channel_id=1, source_target_pairs={{0,24},{8,0},{16,8},{24,16},{1,25},{9,1},{17,9},{25,17},{2,26},{10... | collective-permute-start | bytes 1179656 | tf_op jit(solution)/shard_map/ppermute | solution.py:382
  710.8 39.2 %collective-permute-start.110 = (bf16[1,512,384]{2,1,0:T(8,128)(2,1)}, bf16[1,512,384]{2,1,0:T(8,128)(2,1)S(1)}, u32[]{:S(2)}, u32[]{:S(2)}) collective-permute-start(bf16[1,512,384]{2,1,0:T(8,128)(2,1)} %get-tuple-element.554), channel_id=1, source_target_pairs={{0,16},{8,24},{16,0},{24,8},{1,17},{9,25},{17,1},{25,9},{2,18},{10... | collective-permute-start | bytes 1179656 | tf_op jit(solution)/shard_map/ppermute | solution.py:382
  749.7 55.8 %collective-permute-start.97 = (bf16[2,512,384]{2,1,0:T(8,128)(2,1)}, bf16[2,512,384]{2,1,0:T(8,128)(2,1)S(1)}, u32[]{:S(2)}, u32[]{:S(2)}) collective-permute-start(bf16[2,512,384]{2,1,0:T(8,128)(2,1)} %get-tuple-element.535), channel_id=1, source_target_pairs={{0,8},{8,16},{16,24},{24,0},{1,9},{9,17},{17,25},{25,1},{2,10},{10... | collective-permute-start | bytes 2359304 | tf_op jit(solution)/shard_map/ppermute | solution.py:382
  750.1 56.6 %collective-permute-start.98 = (bf16[2,512,384]{2,1,0:T(8,128)(2,1)}, bf16[2,512,384]{2,1,0:T(8,128)(2,1)S(1)}, u32[]{:S(2)}, u32[]{:S(2)}) collective-permute-start(bf16[2,512,384]{2,1,0:T(8,128)(2,1)} %get-tuple-element.536), channel_id=1, source_target_pairs={{0,16},{8,24},{16,0},{24,8},{1,17},{9,25},{17,1},{25,9},{2,18},{10... | collective-permute-start | bytes 2359304 | tf_op jit(solution)/shard_map/ppermute | solution.py:382
  751.1 58.7 %collective-permute-start.99 = (bf16[2,512,384]{2,1,0:T(8,128)(2,1)}, bf16[2,512,384]{2,1,0:T(8,128)(2,1)}, u32[]{:S(2)}, u32[]{:S(2)}) collective-permute-start(bf16[2,512,384]{2,1,0:T(8,128)(2,1)} %get-tuple-element.537), channel_id=1, source_target_pairs={{0,24},{8,0},{16,8},{24,16},{1,25},{9,1},{17,9},{25,17},{2,26},{10... | collective-permute-start | bytes 2359304 | tf_op jit(solution)/shard_map/ppermute | solution.py:382
  762.8 33.7 %collective-permute-start.111 = (bf16[1,512,384]{2,1,0:T(8,128)(2,1)S(1)}, bf16[1,512,384]{2,1,0:T(8,128)(2,1)S(1)}, u32[]{:S(2)}, u32[]{:S(2)}) collective-permute-start(bf16[1,512,384]{2,1,0:T(8,128)(2,1)S(1)} %copy-done.139), channel_id=1, source_target_pairs={{0,8},{8,16},{16,24},{24,0},{1,9},{9,17},{17,25},{25,1},{2,10},{10... | collective-permute-start | bytes 1179656 | tf_op jit(solution)/shard_map/ppermute | solution.py:382
  762.9 41.6 %collective-permute-start.112 = (bf16[1,512,384]{2,1,0:T(8,128)(2,1)}, bf16[1,512,384]{2,1,0:T(8,128)(2,1)S(1)}, u32[]{:S(2)}, u32[]{:S(2)}) collective-permute-start(bf16[1,512,384]{2,1,0:T(8,128)(2,1)} %get-tuple-element.557), channel_id=1, source_target_pairs={{0,24},{8,0},{16,8},{24,16},{1,25},{9,1},{17,9},{25,17},{2,26},{10... | collective-permute-start | bytes 1179656 | tf_op jit(solution)/shard_map/ppermute | solution.py:382
  796.6 67.3 %collective-permute-start.115 = (bf16[2,512,384]{2,1,0:T(8,128)(2,1)}, bf16[2,512,384]{2,1,0:T(8,128)(2,1)S(1)}, u32[]{:S(2)}, u32[]{:S(2)}) collective-permute-start(bf16[2,512,384]{2,1,0:T(8,128)(2,1)} %get-tuple-element.561), channel_id=1, source_target_pairs={{0,24},{8,0},{16,8},{24,16},{1,25},{9,1},{17,9},{25,17},{2,26},{10... | collective-permute-start | bytes 2359304 | tf_op jit(solution)/shard_map/ppermute | solution.py:382
  804.5 61.0 %collective-permute-start.116 = (bf16[2,512,384]{2,1,0:T(8,128)(2,1)}, bf16[2,512,384]{2,1,0:T(8,128)(2,1)S(1)}, u32[]{:S(2)}, u32[]{:S(2)}) collective-permute-start(bf16[2,512,384]{2,1,0:T(8,128)(2,1)} %get-tuple-element.562), channel_id=1, source_target_pairs={{0,16},{8,24},{16,0},{24,8},{1,17},{9,25},{17,1},{25,9},{2,18},{10... | collective-permute-start | bytes 2359304 | tf_op jit(solution)/shard_map/ppermute | solution.py:382
  805.6 47.9 %collective-permute-start.113 = (bf16[1,512,384]{2,1,0:T(8,128)(2,1)}, bf16[1,512,384]{2,1,0:T(8,128)(2,1)}, u32[]{:S(2)}, u32[]{:S(2)}) collective-permute-start(bf16[1,512,384]{2,1,0:T(8,128)(2,1)} %get-tuple-element.558), channel_id=1, source_target_pairs={{0,16},{8,24},{16,0},{24,8},{1,17},{9,25},{17,1},{25,9},{2,18},{10... | collective-permute-start | bytes 1179656 | tf_op jit(solution)/shard_map/ppermute | solution.py:382
  807.5 60.8 %collective-permute-start.117 = (bf16[2,512,384]{2,1,0:T(8,128)(2,1)}, bf16[2,512,384]{2,1,0:T(8,128)(2,1)S(1)}, u32[]{:S(2)}, u32[]{:S(2)}) collective-permute-start(bf16[2,512,384]{2,1,0:T(8,128)(2,1)} %get-tuple-element.563), channel_id=1, source_target_pairs={{0,8},{8,16},{16,24},{24,0},{1,9},{9,17},{17,25},{25,1},{2,10},{10... | collective-permute-start | bytes 2359304 | tf_op jit(solution)/shard_map/ppermute | solution.py:382
  809.8 46.3 %collective-permute-start.114 = (bf16[1,512,384]{2,1,0:T(8,128)(2,1)}, bf16[1,512,384]{2,1,0:T(8,128)(2,1)}, u32[]{:S(2)}, u32[]{:S(2)}) collective-permute-start(bf16[1,512,384]{2,1,0:T(8,128)(2,1)} %get-tuple-element.559), channel_id=1, source_target_pairs={{0,8},{8,16},{16,24},{24,0},{1,9},{9,17},{17,25},{25,1},{2,10},{10... | collective-permute-start | bytes 1179656 | tf_op jit(solution)/shard_map/ppermute | solution.py:382
  853.5 52.4 %collective-permute-start.118 = (bf16[2,512,384]{2,1,0:T(8,128)(2,1)}, bf16[2,512,384]{2,1,0:T(8,128)(2,1)S(1)}, u32[]{:S(2)}, u32[]{:S(2)}) collective-permute-start(bf16[2,512,384]{2,1,0:T(8,128)(2,1)} %get-tuple-element.565), channel_id=1, source_target_pairs={{0,24},{8,0},{16,8},{24,16},{1,25},{9,1},{17,9},{25,17},{2,26},{10... | collective-permute-start | bytes 2359304 | tf_op jit(solution)/shard_map/ppermute | solution.py:382
  856.0 50.9 %collective-permute-start.119 = (bf16[2,512,384]{2,1,0:T(8,128)(2,1)}, bf16[2,512,384]{2,1,0:T(8,128)(2,1)S(1)}, u32[]{:S(2)}, u32[]{:S(2)}) collective-permute-start(bf16[2,512,384]{2,1,0:T(8,128)(2,1)} %get-tuple-element.566), channel_id=1, source_target_pairs={{0,16},{8,24},{16,0},{24,8},{1,17},{9,25},{17,1},{25,9},{2,18},{10... | collective-permute-start | bytes 2359304 | tf_op jit(solution)/shard_map/ppermute | solution.py:382
  863.8 30.1 %collective-permute-start.92 = (bf16[1,512,384]{2,1,0:T(8,128)(2,1)S(1)}, bf16[1,512,384]{2,1,0:T(8,128)(2,1)S(1)}, u32[]{:S(2)}, u32[]{:S(2)}) collective-permute-start(bf16[1,512,384]{2,1,0:T(8,128)(2,1)S(1)} %copy-done.127), channel_id=1, source_target_pairs={{0,16},{8,24},{16,0},{24,8},{1,17},{9,25},{17,1},{25,9},{2,18},{10... | collective-permute-start | bytes 1179656 | tf_op jit(solution)/shard_map/ppermute | solution.py:382
  865.5 34.0 %collective-permute-start.93 = (bf16[1,512,384]{2,1,0:T(8,128)(2,1)S(1)}, bf16[1,512,384]{2,1,0:T(8,128)(2,1)S(1)}, u32[]{:S(2)}, u32[]{:S(2)}) collective-permute-start(bf16[1,512,384]{2,1,0:T(8,128)(2,1)S(1)} %copy-done.126), channel_id=1, source_target_pairs={{0,24},{8,0},{16,8},{24,16},{1,25},{9,1},{17,9},{25,17},{2,26},{10... | collective-permute-start | bytes 1179656 | tf_op jit(solution)/shard_map/ppermute | solution.py:382
  868.4 42.4 %collective-permute-start.120 = (bf16[2,512,384]{2,1,0:T(8,128)(2,1)S(1)}, bf16[2,512,384]{2,1,0:T(8,128)(2,1)S(1)}, u32[]{:S(2)}, u32[]{:S(2)}) collective-permute-start(bf16[2,512,384]{2,1,0:T(8,128)(2,1)S(1)} %copy-done.125), channel_id=1, source_target_pairs={{0,8},{8,16},{16,24},{24,0},{1,9},{9,17},{17,25},{25,1},{2,10},{10... | collective-permute-start | bytes 2359304 | tf_op jit(solution)/shard_map/ppermute | solution.py:382
  (208 other events, 7291.0 us)

commit v2 on v1

--- a/solution.py
+++ b/solution.py
@@ -16,7 +16,9 @@
 PART = 64
 FINE = 16
 SPAN = 256
-EARLY = 2
+EARLY = 1
+HALVES = 1
+LIMITS = (40,40,40,40)
 NUMBER = 8
 F32 = jnp.float32
 BF16 = jnp.bfloat16
@@ -33,8 +35,8 @@
     return jnp.dot(left, right, preferred_element_type=F32)
 
 
-def params(**extra):
-    return pltpu.CompilerParams(vmem_limit_bytes=56 << 20, **extra)
+def params(mebibytes):
+    return pltpu.CompilerParams(vmem_limit_bytes=mebibytes << 20)
 
 
 def cost(flops, bytes_accessed):
@@ -78,7 +80,7 @@
                 ].astype(BF16)
             return carry
 
-        lax.fori_loop(0, each, one_order, 0, unroll=8)
+        lax.fori_loop(0, each, one_order, 0, unroll=4)
 
 
 def analyse(field, gain, table, parts, first, count):
@@ -96,10 +98,10 @@
         out_specs=[pl.BlockSpec((each, BAND, channels), lambda i: (0, i, 0))] * parts,
         out_shape=[jax.ShapeDtypeStruct((each, count, channels), BF16)] * parts,
         scratch_shapes=[
-            pltpu.VMEM((2, length, channels), BF16),
+            pltpu.VMEM((4, length, channels), BF16),
             pltpu.VMEM((channels // LANES, BAND * orders, LANES), F32),
         ],
-        compiler_params=params(),
+        compiler_params=params(LIMITS[0]),
         cost_estimate=cost(2 * count * orders * length * channels, 3 * count * length * channels),
     )(field, gain, table)
 
@@ -121,7 +123,7 @@
         for part in range(parts):
             slab = slabs[piece * parts + part]
             rows = slab.shape[1]
-            origin = lax.rem(own + parts - part, parts) * total + offsets[piece]
+            origin = lax.bitwise_xor(own, part) * total + offsets[piece]
             place = pl.ds(pl.multiple_of(origin, rows), rows)
             for ri in range(2):
                 spectra[ri, place, :] = slab[ri]
@@ -151,7 +153,7 @@
         for index, (offset, size) in enumerate(targets):
             for part in range(parts):
                 out = outs[index * parts + part]
-                base = lax.rem(own + part, parts) * total + offset
+                base = lax.bitwise_xor(own, part) * total + offset
 
                 def one_row(row, carry, out=out, base=base):
                     for tile in range(channels // LANES):
@@ -160,7 +162,7 @@
                         ].astype(BF16)
                     return carry
 
-                lax.fori_loop(0, size, one_row, 0, unroll=4)
+                lax.fori_loop(0, size, one_row, 0, unroll=2)
 
 
 def spectral(scalars, pieces, forward, inverse, spec_filter, first, number, targets):
@@ -215,7 +217,7 @@
         ),
         out_shape=out_shape,
         input_output_aliases=aliases,
-        compiler_params=params(),
+        compiler_params=params(LIMITS[1]),
         cost_estimate=cost(
             8 * number * degrees * latitudes * channels,
             8 * number * latitudes * channels + 4 * number * degrees * latitudes,
@@ -260,7 +262,7 @@
     share = size // members
 
     def position(r, sc):
-        return lax.rem(sc[1] + r // share, members) * share + lax.rem(r, share)
+        return lax.bitwise_xor(sc[1], r // share) * share + lax.rem(r, share)
 
     def whole(r, sc):
         return (offset + position(r, sc), 0, 0)
@@ -308,7 +310,7 @@
         ),
         out_shape=out_shape,
         input_output_aliases=aliases,
-        compiler_params=params(),
+        compiler_params=params(LIMITS[2]),
         cost_estimate=cost(
             2 * size * length * channels * (table.shape[1] + 2 * hidden),
             8 * size * length * channels,
@@ -372,14 +374,19 @@
         ),
         out_shape=out_shape,
         input_output_aliases={members + 2: 0} if continued else {},
-        compiler_params=params(),
+        compiler_params=params(LIMITS[3]),
         cost_estimate=cost(100 * share * length * channels, 18 * share * length * channels),
     )(scalars, *fields, observed, *([carried] if continued else []))
 
 
-def shift(array, axis, step):
+def swap(array, axis, part):
     size = lax.axis_size(axis)
-    return lax.ppermute(array, axis, [(i, (i + step) % size) for i in range(size)])
+    return lax.ppermute(array, axis, [(i, i ^ part) for i in range(size)])
+
+
+def exchange(slabs, axis):
+    moved = [swap(slabs[part], axis, part) for part in range(len(slabs) - 1, 0, -1)]
+    return [slabs[0]] + moved[::-1]
 
 
 def place(whole, pieces):
@@ -394,12 +401,7 @@
 
 
 def chunk_sizes(rows, unit):
-    units = rows // unit
-    if units < 6:
-        return (unit,) * units
-    middle = units - 4
-    sizes = [1, 1] + [2] * (middle // 2) + [1] * (middle % 2) + [1, 1]
-    return tuple(unit * size for size in sizes)
+    return (unit,) * (rows // unit)
 
 
 def pipelined(
@@ -430,30 +432,30 @@
     waves = wave_of_slot.reshape(parts, groups, number)
     steps = jnp.arange(parts, dtype=jnp.int32)
     columns = jnp.arange(length, dtype=jnp.int32)
-    outgoing = jnp.take(waves, (own + steps) % parts, axis=0).transpose(1, 0, 2)
-    angles = angles_of(outgoing[..., None, None], columns, length)
-    turn = jnp.arange(2, dtype=jnp.int32)[:, None]
-    tables = jnp.where(turn == 0, jnp.cos(angles), -jnp.sin(angles)) * (1.0 / length)
-    tables = tables.astype(BF16).reshape(groups, parts * number * 2, length)
-    incoming = jnp.take(wave_of_slot.reshape(parts, slots), (own - steps) % parts, axis=0)
-    incoming = jnp.repeat(incoming.reshape(-1), 2)
+    waves = jnp.take(waves, own ^ steps, axis=0)
+    turn = (jnp.arange(2, dtype=jnp.int32) == 0)[:, None]
+
+    def outgoing(group):
+        angles = angles_of(waves[:, group, :, None, None], columns, length)
+        table = jnp.where(turn, jnp.cos(angles), -jnp.sin(angles)) * (1.0 / length)
+        return table.astype(BF16).reshape(parts * number * 2, length)
+
+    tables = [outgoing(group) for group in range(groups)]
+    incoming = jnp.repeat(waves.reshape(-1), 2)
     angles = angles_of(incoming[None, :], columns[:, None], length)
     weights = jnp.where(incoming == 0, 1.0, 2.0).astype(F32)[None, :]
     even = (jnp.arange(incoming.shape[0]) % 2 == 0)[None, :]
     back_table = (weights * jnp.where(even, jnp.cos(angles), -jnp.sin(angles))).astype(BF16)
     local_waves = lax.dynamic_slice_in_dim(wave_of_slot, own * slots, slots)
 
-    def spread(slabs):
-        return [slabs[0]] + [shift(slabs[part], "lat", part) for part in range(1, parts)]
-
     received = []
     for group in range(groups):
-        halves = 2 if group == 0 else 1
+        halves = HALVES if group == 0 else 1
         pieces = []
         for half in range(halves):
             count = rows // halves
             slabs = analyse(field, gain_first, tables[group], parts, half * count, count)
-            pieces.append((half * count, spread(slabs)))
+            pieces.append((half * count, exchange(slabs, "lat")))
         received.append(pieces)
     starts = [sum(chunks[:index]) for index in range(len(chunks))]
     early = [None] * EARLY
@@ -487,14 +489,14 @@
         if group == groups - 2:
             arrived = []
             for index in range(EARLY):
-                arrived.append(spread(early[index]))
+                arrived.append(exchange(early[index], "lat"))
 
     predicted = None
     slope = None
     offset = 0
     placed = []
     for index, size in enumerate(chunks):
-        slabs = spread(profiles[index])
+        slabs = exchange(profiles[index], "lat")
         if index < EARLY:
             slabs = [slab for both in zip(arrived[index], slabs) for slab in both]
         predicted, *sends = finish(
@@ -509,15 +511,13 @@
             offset,
             members,
         )
-        fields = [sends[0]] + [
-            shift(sends[part], "member", part) for part in range(1, members)
-        ]
+        fields = exchange(sends, "member")
         slope, *grads = score(scalars, fields, observed, slope, offset)
         share = size // members
-        pieces = []
-        for part in range(1, members):
-            back = shift(grads[part - 1], "member", members - part)
-            pieces.append((back, offset + (own_member + part) % members * share))
+        back = exchange([None] + grads, "member")
+        pieces = [
+            (back[part], offset + (own_member ^ part) * share) for part in range(1, members)
+        ]
         placed.append(pieces)
         offset += size
         if index >= 2:
@@ -573,6 +573,8 @@
     if (
         lat_rows % 16 == 0
         and lat_rows % members == 0
+        and parts & (parts - 1) == 0
+        and members & (members - 1) == 0
         and slots % NUMBER == 0
         and slots >= 2 * NUMBER
         and lat_rows >= 2 * members

time: 946 us -> 983 us (1.039)
  starting transfers between devices: 395 us -> 259 us
  waiting for transfers between devices: 224 us -> 344 us
  local copies, waits for them, and re-layouts: 38.5 us -> 113 us
  Pallas kernels: 266 us -> 246 us
    ppermute x127 -> x139, starting transfers between devices: 395 us -> 259 us  [swap(): return lax.ppermute(array, axis, [(i, i ^ part) for i in range(size)])]
    ppermute x127 -> x139, waiting for transfers between devices: 224 us -> 344 us  [swap(): return lax.ppermute(array, axis, [(i, i ^ part) for i in range(size)])]
    unnamed x290 -> x410, local copies, waits for them, and re-layouts: 10.8 us -> 87.2 us
    pallas_call x6 -> x8, Pallas kernels: 84.3 us -> 74.2 us  [finish(): pl.pallas_call(functools.partial(finish_body, parts, members, carried is...]
    pallas_call x5 -> x4, Pallas kernels: 79.8 us -> 72.8 us  [analyse(): pl.pallas_call(functools.partial(analysis_body, parts), grid=(count // BA...]
    dynamic_update_slice x18 -> x24, local copies, waits for them, and re-layouts: 20.2 us -> 20.8 us  [place(): whole = lax.dynamic_update_slice_in_dim(whole, piece, start, 0)]
    pallas_call x6 -> x8, Pallas kernels: 38.7 us -> 38.5 us  [score(): pl.pallas_call(functools.partial(score_body, members, continued), grid_sp...]
  transfers between devices with their start and end apart: 127 -> 139, of which waited for: 30 -> 46; matrix products, arithmetic and copies ran while one was open for 3% -> 3% of each run, Pallas kernels for 26% -> 23%
where the time goes in v2:
time: 983 us; the launch traced here: 971 us
  waiting for transfers between devices  344 us (35%)
  starting transfers between devices  259 us (26%)
  Pallas kernels  246 us (25%)
  local copies, waits for them, and re-layouts  113 us (11%)
    ppermute x139, waiting for transfers between devices, swap(): return lax.ppermute(array, axis, [(i, i ^ part) for i in range(size)])  344 us
    ppermute x139, starting transfers between devices, swap(): return lax.ppermute(array, axis, [(i, i ^ part) for i in range(size)])  259 us
    unnamed x410, local copies, waits for them, and re-layouts  87.2 us
    pallas_call x8, Pallas kernels, finish(): pl.pallas_call(functools.partial(finish_body, parts, members, carried is...  74.2 us
    pallas_call x4, Pallas kernels, analyse(): pl.pallas_call(functools.partial(analysis_body, parts), grid=(count // BA...  72.8 us
    pallas_call x4, Pallas kernels, spectral(): pl.pallas_call(functools.partial(spectral_body, parts, latitudes // parts...  60.9 us
    pallas_call x8, Pallas kernels, score(): pl.pallas_call(functools.partial(score_body, members, continued), grid_sp...  38.5 us
    dynamic_update_slice x24, local copies, waits for them, and re-layouts, place(): whole = lax.dynamic_update_slice_in_dim(whole, piece, start, 0)  20.8 us
  transfers between devices with their start and end apart: 139, of which 46 were waited for; matrix products, arithmetic and copies ran while one was open for 3% of the time, Pallas kernels for 23%

profile of v2, /device:TPU:0, one launch (start us, length us, event | category | flops | bytes accessed | tf_op | source)
XLA Modules:
  0.0 971.3 jit_solution(2873711109325387313)
XLA Ops:
  7.9 18.5 %shard_map.113 = (bf16[16,32,384]{2,1,0:T(8,128)(2,1)S(1)}, bf16[16,32,384]{2,1,0:T(8,128)(2,1)S(1)}, bf16[16,32,384]{2,1,0:T(8,128)(2,1)S(1)}, bf16[16,32,384]{...) custom-call(bf16[32,512,384]{2,1,0:T(8,128)(2,1)} %bitcast.29, ...), custom_call_target="tpu_custom_call" | custom-call | flops 1610612736 | bytes 18874368 | tf_op jit(solution)/shard_map/pallas_call | solution.py:90
  30.2 17.7 %shard_map.114 = (bf16[16,32,384]{2,1,0:T(8,128)(2,1)S(1)}, bf16[16,32,384]{2,1,0:T(8,128)(2,1)S(1)}, bf16[16,32,384]{2,1,0:T(8,128)(2,1)S(1)}, bf16[16,32,384]{...) custom-call(bf16[32,512,384]{2,1,0:T(8,128)(2,1)} %bitcast.30, ...), custom_call_target="tpu_custom_call" | custom-call | flops 1610612736 | bytes 18874368 | tf_op jit(solution)/shard_map/pallas_call | solution.py:90
  56.6 18.3 %shard_map.115 = (bf16[16,32,384]{2,1,0:T(8,128)(2,1)S(1)}, bf16[16,32,384]{2,1,0:T(8,128)(2,1)S(1)}, bf16[16,32,384]{2,1,0:T(8,128)(2,1)S(1)}, bf16[16,32,384]{...) custom-call(bf16[32,512,384]{2,1,0:T(8,128)(2,1)} %bitcast.31, ...), custom_call_target="tpu_custom_call" | custom-call | flops 1610612736 | bytes 18874368 | tf_op jit(solution)/shard_map/pallas_call | solution.py:90
  77.1 7.1 collective-permute-done.9.refs_3_
  84.9 19.4 %collective-permute-done.11.refs_5_ = bf16[16,32,384]{2,1,0:T(8,128)(2,1)S(1)} collective-permute-done((bf16[16,32,384]{2,1,0:T(8,128)(2,1)S(1)}, bf16[16,32,384]{2,1,0:T(8,128)(2,1)S(1)}, u32[]{:S(2)}, u32[]{:S(2)}) %collective-permute-start.11) | collective-permute-done | bytes 393248 | tf_op jit(solution)/shard_map/ppermute | solution.py:384
  104.4 11.3 %collective-permute-start.17 = (bf16[16,32,384]{2,1,0:T(8,128)(2,1)S(1)}, bf16[16,32,384]{2,1,0:T(8,128)(2,1)S(1)}, u32[]{:S(2)}, u32[]{:S(2)}) collective-permute-start(bf16[16,32,384]{2,1,0:T(8,128)(2,1)S(1)} %get-tuple-element.382), channel_id=1, source_target_pairs={{0,4},{1,5},{2,6},{3,7},{4,0},{5,1},{6,2},{7,3},{8,12},{9,13},{10,... | collective-permute-start | bytes 1179656 | tf_op jit(solution)/shard_map/ppermute | solution.py:384
  115.7 18.3 %shard_map.116 = (bf16[16,32,384]{2,1,0:T(8,128)(2,1)S(1)}, bf16[16,32,384]{2,1,0:T(8,128)(2,1)}, bf16[16,32,384]{2,1,0:T(8,128)(2,1)}, bf16[16,32,384]{2,1,0:T(...) custom-call(bf16[32,512,384]{2,1,0:T(8,128)(2,1)} %bitcast.32, ...), custom_call_target="tpu_custom_call" | custom-call | flops 1610612736 | bytes 18874368 | tf_op jit(solution)/shard_map/pallas_call | solution.py:90
  141.1 23.6 %collective-permute-done.17.refs_4_ = bf16[16,32,384]{2,1,0:T(8,128)(2,1)S(1)} collective-permute-done((bf16[16,32,384]{2,1,0:T(8,128)(2,1)S(1)}, bf16[16,32,384]{2,1,0:T(8,128)(2,1)S(1)}, u32[]{:S(2)}, u32[]{:S(2)}) %collective-permute-start.17) | collective-permute-done | bytes 393248 | tf_op jit(solution)/shard_map/ppermute | solution.py:384
  165.6 6.7 collective-permute-done.18.refs_5_
  173.0 10.3 %collective-permute-start.24 = (bf16[16,32,384]{2,1,0:T(8,128)(2,1)}, bf16[16,32,384]{2,1,0:T(8,128)(2,1)S(1)}, u32[]{:S(2)}, u32[]{:S(2)}) collective-permute-start(bf16[16,32,384]{2,1,0:T(8,128)(2,1)} %get-tuple-element.390), channel_id=1, source_target_pairs={{0,4},{1,5},{2,6},{3,7},{4,0},{5,1},{6,2},{7,3},{8,12},{9,13},{10,... | collective-permute-start | bytes 1179656 | tf_op jit(solution)/shard_map/ppermute | solution.py:384
  183.2 16.3 %collective-permute-start.25 = (bf16[16,32,384]{2,1,0:T(8,128)(2,1)S(1)}, bf16[16,32,384]{2,1,0:T(8,128)(2,1)S(1)}, u32[]{:S(2)}, u32[]{:S(2)}) collective-permute-start(bf16[16,32,384]{2,1,0:T(8,128)(2,1)S(1)} %get-tuple-element.391), channel_id=1, source_target_pairs={{0,5},{1,4},{2,7},{3,6},{4,1},{5,0},{6,3},{7,2},{8,13},{9,12},{10,... | collective-permute-start | bytes 1179656 | tf_op jit(solution)/shard_map/ppermute | solution.py:384
  204.9 27.3 %collective-permute-done.24.refs_4_ = bf16[16,32,384]{2,1,0:T(8,128)(2,1)S(1)} collective-permute-done((bf16[16,32,384]{2,1,0:T(8,128)(2,1)}, bf16[16,32,384]{2,1,0:T(8,128)(2,1)S(1)}, u32[]{:S(2)}, u32[]{:S(2)}) %collective-permute-start.24) | collective-permute-done | bytes 393248 | tf_op jit(solution)/shard_map/ppermute | solution.py:384
  233.0 15.1 %collective-permute-done.25.refs_5_ = bf16[16,32,384]{2,1,0:T(8,128)(2,1)S(1)} collective-permute-done((bf16[16,32,384]{2,1,0:T(8,128)(2,1)S(1)}, bf16[16,32,384]{2,1,0:T(8,128)(2,1)S(1)}, u32[]{:S(2)}, u32[]{:S(2)}) %collective-permute-start.25) | collective-permute-done | bytes 393248 | tf_op jit(solution)/shard_map/ppermute | solution.py:384
  258.8 15.6 %shard_map.117 = (bf16[4,48,384]{2,1,0:T(8,128)(2,1)S(1)}, bf16[4,48,384]{2,1,0:T(8,128)(2,1)S(1)}, bf16[4,48,384]{2,1,0:T(8,128)(2,1)S(1)}, bf16[4,48,384]{2,1,...) custom-call(s32[10]{0:T(128)S(1)} %get-tuple-element.722.scalars, ...), custom_call_target="tpu_custom_call" | custom-call | flops 1610612736 | bytes 8388608 | tf_op jit(solution)/shard_map/pallas_call | solution.py:199
  275.7 15.1 %shard_map.118 = (bf16[4,48,384]{2,1,0:T(8,128)(2,1)S(1)}, bf16[4,48,384]{2,1,0:T(8,128)(2,1)S(1)}, bf16[4,48,384]{2,1,0:T(8,128)(2,1)S(1)}, bf16[4,48,384]{2,1,...) custom-call(s32[10]{0:T(128)S(1)} %get-tuple-element.740.scalars, ...), custom_call_target="tpu_custom_call", output_to_operand_aliasing={{0}: (12, {}), {1}: (13, {}), {2}: (14, {}), {3}: (15, {}),... | custom-call | flops 1610612736 | bytes 8388608 | tf_op jit(solution)/shard_map/pallas_call | solution.py:199
  290.8 15.2 %shard_map.119 = (bf16[4,48,384]{2,1,0:T(8,128)(2,1)S(1)}, bf16[4,48,384]{2,1,0:T(8,128)(2,1)S(1)}, bf16[4,48,384]{2,1,0:T(8,128)(2,1)S(1)}, bf16[4,48,384]{2,1,...) custom-call(s32[10]{0:T(128)S(1)} %get-tuple-element.741.scalars, ...), custom_call_target="tpu_custom_call", output_to_operand_aliasing={{0}: (12, {}), {1}: (13, {}), {2}: (14, {}), {3}: (15, {}),... | custom-call | flops 1610612736 | bytes 8388608 | tf_op jit(solution)/shard_map/pallas_call | solution.py:199
  307.1 15.0 %shard_map.120 = (bf16[4,16,384]{2,1,0:T(8,128)(2,1)S(1)}, bf16[4,16,384]{2,1,0:T(8,128)(2,1)S(1)}, bf16[4,16,384]{2,1,0:T(8,128)(2,1)S(1)}, bf16[4,16,384]{2,1,...) custom-call(s32[10]{0:T(128)S(1)} %get-tuple-element.742.scalars, ...), custom_call_target="tpu_custom_call", output_to_operand_aliasing={{8}: (12, {}), {9}: (13, {}), {10}: (14, {}), {11}: (15, {}... | custom-call | flops 1610612736 | bytes 8388608 | tf_op jit(solution)/shard_map/pallas_call | solution.py:199
  352.0 39.4 %collective-permute-start.80 = (bf16[4,16,384]{2,1,0:T(8,128)(2,1)S(1)}, bf16[4,16,384]{2,1,0:T(8,128)(2,1)S(1)}, u32[]{:S(2)}, u32[]{:S(2)}) collective-permute-start(bf16[4,16,384]{2,1,0:T(8,128)(2,1)S(1)} %get-tuple-element.639), channel_id=1, source_target_pairs={{0,2},{1,3},{2,0},{3,1},{4,6},{5,7},{6,4},{7,5},{8,10},{9,11},{10,... | collective-permute-start | bytes 147464 | tf_op jit(solution)/shard_map/ppermute | solution.py:384
  412.6 7.5 collective-permute-done.83.refs_8_
  426.2 7.6 collective-permute-done.89.refs_14_
  434.6 3.1 collective-permute-start.43
  440.7 3.0 collective-permute-done.43.refs_2_
  449.9 4.3 multiply_convert_fusion.refs_17_.refs_9_
  459.3 8.7 collective-permute-done.71.refs_2_
  481.2 9.2 shard_map.121
  496.8 9.4 shard_map.122
  506.3 9.9 %collective-permute-done.66.refs_4_ = bf16[4,64,384]{2,1,0:T(8,128)(2,1)S(1)} collective-permute-done((bf16[4,64,384]{2,1,0:T(8,128)(2,1)S(1)}, bf16[4,64,384]{2,1,0:T(8,128)(2,1)S(1)}, u32[]{:S(2)}, u32[]{:S(2)}) %collective-permute-start.66) | collective-permute-done | bytes 196640 | tf_op jit(solution)/shard_map/ppermute | solution.py:384
  516.3 8.1 collective-permute-done.67.refs_5_
  527.8 9.6 shard_map.123
  537.4 19.0 %collective-permute-start.51 = (bf16[4,64,384]{2,1,0:T(8,128)(2,1)S(1)}, bf16[4,64,384]{2,1,0:T(8,128)(2,1)S(1)}, u32[]{:S(2)}, u32[]{:S(2)}) collective-permute-start(bf16[4,64,384]{2,1,0:T(8,128)(2,1)S(1)} %copy-done.34), channel_id=1, source_target_pairs={{0,3},{1,2},{2,1},{3,0},{4,7},{5,6},{6,5},{7,4},{8,11},{9,10},{10,... | collective-permute-start | bytes 589832 | tf_op jit(solution)/shard_map/ppermute | solution.py:384
  562.7 9.2 shard_map.124
  573.6 10.1 %collective-permute-done.52.refs_4_ = bf16[4,64,384]{2,1,0:T(8,128)(2,1)S(1)} collective-permute-done((bf16[4,64,384]{2,1,0:T(8,128)(2,1)S(1)}, bf16[4,64,384]{2,1,0:T(8,128)(2,1)S(1)}, u32[]{:S(2)}, u32[]{:S(2)}) %collective-permute-start.52) | collective-permute-done | bytes 196640 | tf_op jit(solution)/shard_map/ppermute | solution.py:384
  583.7 8.1 collective-permute-done.53.refs_5_
  595.3 9.2 shard_map.125
  605.2 19.0 %collective-permute-start.37 = (bf16[4,64,384]{2,1,0:T(8,128)(2,1)S(1)}, bf16[4,64,384]{2,1,0:T(8,128)(2,1)S(1)}, u32[]{:S(2)}, u32[]{:S(2)}) collective-permute-start(bf16[4,64,384]{2,1,0:T(8,128)(2,1)S(1)} %copy-done.56), channel_id=1, source_target_pairs={{0,3},{1,2},{2,1},{3,0},{4,7},{5,6},{6,5},{7,4},{8,11},{9,10},{10,... | collective-permute-start | bytes 589832 | tf_op jit(solution)/shard_map/ppermute | solution.py:384
  630.5 9.2 shard_map.126
  641.1 10.1 %collective-permute-done.38.refs_4_ = bf16[4,64,384]{2,1,0:T(8,128)(2,1)S(1)} collective-permute-done((bf16[4,64,384]{2,1,0:T(8,128)(2,1)S(1)}, bf16[4,64,384]{2,1,0:T(8,128)(2,1)S(1)}, u32[]{:S(2)}, u32[]{:S(2)}) %collective-permute-start.38) | collective-permute-done | bytes 196640 | tf_op jit(solution)/shard_map/ppermute | solution.py:384
  651.2 8.1 collective-permute-done.39.refs_5_
  662.7 9.3 shard_map.127
  675.0 9.9 %collective-permute-done.31.refs_4_ = bf16[4,64,384]{2,1,0:T(8,128)(2,1)S(1)} collective-permute-done((bf16[4,64,384]{2,1,0:T(8,128)(2,1)S(1)}, bf16[4,64,384]{2,1,0:T(8,128)(2,1)S(1)}, u32[]{:S(2)}, u32[]{:S(2)}) %collective-permute-start.31) | collective-permute-done | bytes 196640 | tf_op jit(solution)/shard_map/ppermute | solution.py:384
  695.8 10.1 %collective-permute-done.113.refs_2_ = bf16[1,512,384]{2,1,0:T(8,128)(2,1)S(1)} collective-permute-done((bf16[1,512,384]{2,1,0:T(8,128)(2,1)S(1)}, bf16[1,512,384]{2,1,0:T(8,128)(2,1)S(1)}, u32[]{:S(2)}, u32[]{:S(2)}) %collective-permute-start.113) | collective-permute-done | bytes 393248 | tf_op jit(solution)/shard_map/ppermute | solution.py:384
  711.4 2.9 collective-permute-done.95.refs_2_
  715.8 3.5 collective-permute-done.97.refs_1_
  738.4 5.1 shard_map.129
  744.2 3.8 collective-permute-done.104.refs_2_
  755.3 9.7 collective-permute-done.110.refs_2_
  772.5 4.8 shard_map.130
  777.7 4.1 collective-permute-done.107.refs_2_
  787.5 19.7 %collective-permute-done.116 = bf16[1,512,384]{2,1,0:T(8,128)(2,1)} collective-permute-done((bf16[1,512,384]{2,1,0:T(8,128)(2,1)}, bf16[1,512,384]{2,1,0:T(8,128)(2,1)}, u32[]{:S(2)}, u32[]{:S(2)}) %collective-permute-start.116) | collective-permute-done | bytes 393248 | tf_op jit(solution)/shard_map/ppermute | solution.py:384
  809.6 9.2 shard_map.128
  818.8 5.0 shard_map.131
  828.8 4.7 shard_map.132
  842.4 4.7 shard_map.133
  848.4 14.9 %collective-permute-done.122 = bf16[1,512,384]{2,1,0:T(8,128)(2,1)S(1)} collective-permute-done((bf16[1,512,384]{2,1,0:T(8,128)(2,1)S(1)}, bf16[1,512,384]{2,1,0:T(8,128)(2,1)S(1)}, u32[]{:S(2)}, u32[]{:S(2)}) %collective-permute-start.122) | collective-permute-done | bytes 393248 | tf_op jit(solution)/shard_map/ppermute | solution.py:384
  868.4 4.7 shard_map.134
  873.2 11.9 %collective-permute-done.125 = bf16[1,512,384]{2,1,0:T(8,128)(2,1)S(1)} collective-permute-done((bf16[1,512,384]{2,1,0:T(8,128)(2,1)S(1)}, bf16[1,512,384]{2,1,0:T(8,128)(2,1)S(1)}, u32[]{:S(2)}, u32[]{:S(2)}) %collective-permute-start.125) | collective-permute-done | bytes 393248 | tf_op jit(solution)/shard_map/ppermute | solution.py:384
  891.6 10.3 %collective-permute-done.128 = bf16[1,512,384]{2,1,0:T(8,128)(2,1)S(1)} collective-permute-done((bf16[1,512,384]{2,1,0:T(8,128)(2,1)S(1)}, bf16[1,512,384]{2,1,0:T(8,128)(2,1)S(1)}, u32[]{:S(2)}, u32[]{:S(2)}) %collective-permute-start.128) | collective-permute-done | bytes 393248 | tf_op jit(solution)/shard_map/ppermute | solution.py:384
  904.6 4.7 shard_map.135
  913.3 5.5 collective-permute-done.92.refs_2_
  920.8 4.7 shard_map.136
  927.8 7.9 collective-permute-done.131
  942.5 10.0 %collective-permute-done.134 = bf16[1,512,384]{2,1,0:T(8,128)(2,1)S(1)} collective-permute-done((bf16[1,512,384]{2,1,0:T(8,128)(2,1)S(1)}, bf16[1,512,384]{2,1,0:T(8,128)(2,1)S(1)}, u32[]{:S(2)}, u32[]{:S(2)}) %collective-permute-start.134) | collective-permute-done | bytes 393248 | tf_op jit(solution)/shard_map/ppermute | solution.py:384
  954.1 3.0 collective-permute-done.136
  957.8 11.4 %collective-permute-done.137 = bf16[1,512,384]{2,1,0:T(8,128)(2,1)S(1)} collective-permute-done((bf16[1,512,384]{2,1,0:T(8,128)(2,1)S(1)}, bf16[1,512,384]{2,1,0:T(8,128)(2,1)S(1)}, u32[]{:S(2)}, u32[]{:S(2)}) %collective-permute-start.137) | collective-permute-done | bytes 393248 | tf_op jit(solution)/shard_map/ppermute | solution.py:384
  (716 shorter events, 280.6 us)
Async XLA Ops:
  49.2 34.9 %collective-permute-start.9 = (bf16[16,32,384]{2,1,0:T(8,128)(2,1)S(1)}, bf16[16,32,384]{2,1,0:T(8,128)(2,1)S(1)}, u32[]{:S(2)}, u32[]{:S(2)}) collective-permute-start(bf16[16,32,384]{2,1,0:T(8,128)(2,1)S(1)} %get-tuple-element.373), channel_id=1, source_target_pairs={{0,3},{1,2},{2,1},{3,0},{4,7},{5,6},{6,5},{7,4},{8,11},{9,10},{10,... | collective-permute-start | bytes 1179656 | tf_op jit(solution)/shard_map/ppermute | solution.py:384
  50.5 34.4 %collective-permute-start.10 = (bf16[16,32,384]{2,1,0:T(8,128)(2,1)S(1)}, bf16[16,32,384]{2,1,0:T(8,128)(2,1)S(1)}, u32[]{:S(2)}, u32[]{:S(2)}) collective-permute-start(bf16[16,32,384]{2,1,0:T(8,128)(2,1)S(1)} %get-tuple-element.374), channel_id=1, source_target_pairs={{0,4},{1,5},{2,6},{3,7},{4,0},{5,1},{6,2},{7,3},{8,12},{9,13},{10,... | collective-permute-start | bytes 1179656 | tf_op jit(solution)/shard_map/ppermute | solution.py:384
  53.1 51.2 %collective-permute-start.11 = (bf16[16,32,384]{2,1,0:T(8,128)(2,1)S(1)}, bf16[16,32,384]{2,1,0:T(8,128)(2,1)S(1)}, u32[]{:S(2)}, u32[]{:S(2)}) collective-permute-start(bf16[16,32,384]{2,1,0:T(8,128)(2,1)S(1)} %get-tuple-element.375), channel_id=1, source_target_pairs={{0,5},{1,4},{2,7},{3,6},{4,1},{5,0},{6,3},{7,2},{8,13},{9,12},{10,... | collective-permute-start | bytes 1179656 | tf_op jit(solution)/shard_map/ppermute | solution.py:384
  54.1 50.3 %collective-permute-start.12 = (bf16[16,32,384]{2,1,0:T(8,128)(2,1)S(1)}, bf16[16,32,384]{2,1,0:T(8,128)(2,1)S(1)}, u32[]{:S(2)}, u32[]{:S(2)}) collective-permute-start(bf16[16,32,384]{2,1,0:T(8,128)(2,1)S(1)} %get-tuple-element.376), channel_id=1, source_target_pairs={{0,6},{1,7},{2,4},{3,5},{4,2},{5,3},{6,0},{7,1},{8,14},{9,15},{10,... | collective-permute-start | bytes 1179656 | tf_op jit(solution)/shard_map/ppermute | solution.py:384
  77.1 57.7 %collective-permute-start.13 = (bf16[16,32,384]{2,1,0:T(8,128)(2,1)S(1)}, bf16[16,32,384]{2,1,0:T(8,128)(2,1)S(1)}, u32[]{:S(2)}, u32[]{:S(2)}) collective-permute-start(bf16[16,32,384]{2,1,0:T(8,128)(2,1)S(1)} %get-tuple-element.377), channel_id=1, source_target_pairs={{0,7},{1,6},{2,5},{3,4},{4,3},{5,2},{6,1},{7,0},{8,15},{9,14},{10,... | collective-permute-start | bytes 1179656 | tf_op jit(solution)/shard_map/ppermute | solution.py:384
  84.1 50.6 %collective-permute-start.14 = (bf16[16,32,384]{2,1,0:T(8,128)(2,1)S(1)}, bf16[16,32,384]{2,1,0:T(8,128)(2,1)S(1)}, u32[]{:S(2)}, u32[]{:S(2)}) collective-permute-start(bf16[16,32,384]{2,1,0:T(8,128)(2,1)S(1)} %get-tuple-element.379), channel_id=1, source_target_pairs={{0,1},{1,0},{2,3},{3,2},{4,5},{5,4},{6,7},{7,6},{8,9},{9,8},{10,11... | collective-permute-start | bytes 1179656 | tf_op jit(solution)/shard_map/ppermute | solution.py:384
  84.9 52.0 %collective-permute-start.15 = (bf16[16,32,384]{2,1,0:T(8,128)(2,1)S(1)}, bf16[16,32,384]{2,1,0:T(8,128)(2,1)S(1)}, u32[]{:S(2)}, u32[]{:S(2)}) collective-permute-start(bf16[16,32,384]{2,1,0:T(8,128)(2,1)S(1)} %get-tuple-element.380), channel_id=1, source_target_pairs={{0,2},{1,3},{2,0},{3,1},{4,6},{5,7},{6,4},{7,5},{8,10},{9,11},{10,... | collective-permute-start | bytes 1179656 | tf_op jit(solution)/shard_map/ppermute | solution.py:384
  104.4 36.0 %collective-permute-start.16 = (bf16[16,32,384]{2,1,0:T(8,128)(2,1)S(1)}, bf16[16,32,384]{2,1,0:T(8,128)(2,1)S(1)}, u32[]{:S(2)}, u32[]{:S(2)}) collective-permute-start(bf16[16,32,384]{2,1,0:T(8,128)(2,1)S(1)} %get-tuple-element.381), channel_id=1, source_target_pairs={{0,3},{1,2},{2,1},{3,0},{4,7},{5,6},{6,5},{7,4},{8,11},{9,10},{10,... | collective-permute-start | bytes 1179656 | tf_op jit(solution)/shard_map/ppermute | solution.py:384
  104.4 60.3 %collective-permute-start.17 = (bf16[16,32,384]{2,1,0:T(8,128)(2,1)S(1)}, bf16[16,32,384]{2,1,0:T(8,128)(2,1)S(1)}, u32[]{:S(2)}, u32[]{:S(2)}) collective-permute-start(bf16[16,32,384]{2,1,0:T(8,128)(2,1)S(1)} %get-tuple-element.382), channel_id=1, source_target_pairs={{0,4},{1,5},{2,6},{3,7},{4,0},{5,1},{6,2},{7,3},{8,12},{9,13},{10,... | collective-permute-start | bytes 1179656 | tf_op jit(solution)/shard_map/ppermute | solution.py:384
  134.7 37.5 %collective-permute-start.18 = (bf16[16,32,384]{2,1,0:T(8,128)(2,1)}, bf16[16,32,384]{2,1,0:T(8,128)(2,1)S(1)}, u32[]{:S(2)}, u32[]{:S(2)}) collective-permute-start(bf16[16,32,384]{2,1,0:T(8,128)(2,1)} %get-tuple-element.383), channel_id=1, source_target_pairs={{0,5},{1,4},{2,7},{3,6},{4,1},{5,0},{6,3},{7,2},{8,13},{9,12},{10,... | collective-permute-start | bytes 1179656 | tf_op jit(solution)/shard_map/ppermute | solution.py:384
  135.6 37.4 %collective-permute-start.19 = (bf16[16,32,384]{2,1,0:T(8,128)(2,1)S(1)}, bf16[16,32,384]{2,1,0:T(8,128)(2,1)}, u32[]{:S(2)}, u32[]{:S(2)}) collective-permute-start(bf16[16,32,384]{2,1,0:T(8,128)(2,1)S(1)} %get-tuple-element.384), channel_id=1, source_target_pairs={{0,6},{1,7},{2,4},{3,5},{4,2},{5,3},{6,0},{7,1},{8,14},{9,15},{10,... | collective-permute-start | bytes 1179656 | tf_op jit(solution)/shard_map/ppermute | solution.py:384
  137.7 45.6 %collective-permute-start.20 = (bf16[16,32,384]{2,1,0:T(8,128)(2,1)S(1)}, bf16[16,32,384]{2,1,0:T(8,128)(2,1)}, u32[]{:S(2)}, u32[]{:S(2)}) collective-permute-start(bf16[16,32,384]{2,1,0:T(8,128)(2,1)S(1)} %get-tuple-element.385), channel_id=1, source_target_pairs={{0,7},{1,6},{2,5},{3,4},{4,3},{5,2},{6,1},{7,0},{8,15},{9,14},{10,... | collective-permute-start | bytes 1179656 | tf_op jit(solution)/shard_map/ppermute | solution.py:384
  141.1 58.4 %collective-permute-start.21 = (bf16[16,32,384]{2,1,0:T(8,128)(2,1)}, bf16[16,32,384]{2,1,0:T(8,128)(2,1)S(1)}, u32[]{:S(2)}, u32[]{:S(2)}) collective-permute-start(bf16[16,32,384]{2,1,0:T(8,128)(2,1)} %get-tuple-element.387), channel_id=1, source_target_pairs={{0,1},{1,0},{2,3},{3,2},{4,5},{5,4},{6,7},{7,6},{8,9},{9,8},{10,11... | collective-permute-start | bytes 1179656 | tf_op jit(solution)/shard_map/ppermute | solution.py:384
  165.4 36.2 %collective-permute-start.22 = (bf16[16,32,384]{2,1,0:T(8,128)(2,1)}, bf16[16,32,384]{2,1,0:T(8,128)(2,1)S(1)}, u32[]{:S(2)}, u32[]{:S(2)}) collective-permute-start(bf16[16,32,384]{2,1,0:T(8,128)(2,1)} %get-tuple-element.388), channel_id=1, source_target_pairs={{0,2},{1,3},{2,0},{3,1},{4,6},{5,7},{6,4},{7,5},{8,10},{9,11},{10,... | collective-permute-start | bytes 1179656 | tf_op jit(solution)/shard_map/ppermute | solution.py:384
  173.0 31.2 %collective-permute-start.23 = (bf16[16,32,384]{2,1,0:T(8,128)(2,1)}, bf16[16,32,384]{2,1,0:T(8,128)(2,1)S(1)}, u32[]{:S(2)}, u32[]{:S(2)}) collective-permute-start(bf16[16,32,384]{2,1,0:T(8,128)(2,1)} %get-tuple-element.389), channel_id=1, source_target_pairs={{0,3},{1,2},{2,1},{3,0},{4,7},{5,6},{6,5},{7,4},{8,11},{9,10},{10,... | collective-permute-start | bytes 1179656 | tf_op jit(solution)/shard_map/ppermute | solution.py:384
  173.0 59.2 %collective-permute-start.24 = (bf16[16,32,384]{2,1,0:T(8,128)(2,1)}, bf16[16,32,384]{2,1,0:T(8,128)(2,1)S(1)}, u32[]{:S(2)}, u32[]{:S(2)}) collective-permute-start(bf16[16,32,384]{2,1,0:T(8,128)(2,1)} %get-tuple-element.390), channel_id=1, source_target_pairs={{0,4},{1,5},{2,6},{3,7},{4,0},{5,1},{6,2},{7,3},{8,12},{9,13},{10,... | collective-permute-start | bytes 1179656 | tf_op jit(solution)/shard_map/ppermute | solution.py:384
  183.2 64.8 %collective-permute-start.25 = (bf16[16,32,384]{2,1,0:T(8,128)(2,1)S(1)}, bf16[16,32,384]{2,1,0:T(8,128)(2,1)S(1)}, u32[]{:S(2)}, u32[]{:S(2)}) collective-permute-start(bf16[16,32,384]{2,1,0:T(8,128)(2,1)S(1)} %get-tuple-element.391), channel_id=1, source_target_pairs={{0,5},{1,4},{2,7},{3,6},{4,1},{5,0},{6,3},{7,2},{8,13},{9,12},{10,... | collective-permute-start | bytes 1179656 | tf_op jit(solution)/shard_map/ppermute | solution.py:384
  200.3 48.5 %collective-permute-start.26 = (bf16[16,32,384]{2,1,0:T(8,128)(2,1)S(1)}, bf16[16,32,384]{2,1,0:T(8,128)(2,1)S(1)}, u32[]{:S(2)}, u32[]{:S(2)}) collective-permute-start(bf16[16,32,384]{2,1,0:T(8,128)(2,1)S(1)} %get-tuple-element.392), channel_id=1, source_target_pairs={{0,6},{1,7},{2,4},{3,5},{4,2},{5,3},{6,0},{7,1},{8,14},{9,15},{10,... | collective-permute-start | bytes 1179656 | tf_op jit(solution)/shard_map/ppermute | solution.py:384
  202.4 49.0 %collective-permute-start.27 = (bf16[16,32,384]{2,1,0:T(8,128)(2,1)S(1)}, bf16[16,32,384]{2,1,0:T(8,128)(2,1)S(1)}, u32[]{:S(2)}, u32[]{:S(2)}) collective-permute-start(bf16[16,32,384]{2,1,0:T(8,128)(2,1)S(1)} %get-tuple-element.393), channel_id=1, source_target_pairs={{0,7},{1,6},{2,5},{3,4},{4,3},{5,2},{6,1},{7,0},{8,15},{9,14},{10,... | collective-permute-start | bytes 1179656 | tf_op jit(solution)/shard_map/ppermute | solution.py:384
  204.9 101.8 %collective-permute-start.2 = (bf16[16,32,384]{2,1,0:T(8,128)(2,1)}, bf16[16,32,384]{2,1,0:T(8,128)(2,1)S(1)}, u32[]{:S(2)}, u32[]{:S(2)}) collective-permute-start(bf16[16,32,384]{2,1,0:T(8,128)(2,1)} %get-tuple-element.365), channel_id=1, source_target_pairs={{0,3},{1,2},{2,1},{3,0},{4,7},{5,6},{6,5},{7,4},{8,11},{9,10},{10,... | collective-permute-start | bytes 1179656 | tf_op jit(solution)/shard_map/ppermute | solution.py:384
  233.0 73.9 %collective-permute-start.3 = (bf16[16,32,384]{2,1,0:T(8,128)(2,1)}, bf16[16,32,384]{2,1,0:T(8,128)(2,1)S(1)}, u32[]{:S(2)}, u32[]{:S(2)}) collective-permute-start(bf16[16,32,384]{2,1,0:T(8,128)(2,1)} %get-tuple-element.366), channel_id=1, source_target_pairs={{0,4},{1,5},{2,6},{3,7},{4,0},{5,1},{6,2},{7,3},{8,12},{9,13},{10,... | collective-permute-start | bytes 1179656 | tf_op jit(solution)/shard_map/ppermute | solution.py:384
  248.8 58.2 %collective-permute-start.4 = (bf16[16,32,384]{2,1,0:T(8,128)(2,1)}, bf16[16,32,384]{2,1,0:T(8,128)(2,1)S(1)}, u32[]{:S(2)}, u32[]{:S(2)}) collective-permute-start(bf16[16,32,384]{2,1,0:T(8,128)(2,1)} %get-tuple-element.367), channel_id=1, source_target_pairs={{0,5},{1,4},{2,7},{3,6},{4,1},{5,0},{6,3},{7,2},{8,13},{9,12},{10,... | collective-permute-start | bytes 1179656 | tf_op jit(solution)/shard_map/ppermute | solution.py:384
  248.8 58.2 %collective-permute-start.5 = (bf16[16,32,384]{2,1,0:T(8,128)(2,1)}, bf16[16,32,384]{2,1,0:T(8,128)(2,1)S(1)}, u32[]{:S(2)}, u32[]{:S(2)}) collective-permute-start(bf16[16,32,384]{2,1,0:T(8,128)(2,1)} %get-tuple-element.368), channel_id=1, source_target_pairs={{0,6},{1,7},{2,4},{3,5},{4,2},{5,3},{6,0},{7,1},{8,14},{9,15},{10,... | collective-permute-start | bytes 1179656 | tf_op jit(solution)/shard_map/ppermute | solution.py:384
  251.4 55.7 %collective-permute-start.6 = (bf16[16,32,384]{2,1,0:T(8,128)(2,1)}, bf16[16,32,384]{2,1,0:T(8,128)(2,1)S(1)}, u32[]{:S(2)}, u32[]{:S(2)}) collective-permute-start(bf16[16,32,384]{2,1,0:T(8,128)(2,1)} %get-tuple-element.369), channel_id=1, source_target_pairs={{0,7},{1,6},{2,5},{3,4},{4,3},{5,2},{6,1},{7,0},{8,15},{9,14},{10,... | collective-permute-start | bytes 1179656 | tf_op jit(solution)/shard_map/ppermute | solution.py:384
  306.7 99.7 %collective-permute-start.77 = (bf16[4,48,384]{2,1,0:T(8,128)(2,1)S(1)}, bf16[4,48,384]{2,1,0:T(8,128)(2,1)S(1)}, u32[]{:S(2)}, u32[]{:S(2)}) collective-permute-start(bf16[4,48,384]{2,1,0:T(8,128)(2,1)S(1)} %get-tuple-element.636), channel_id=1, source_target_pairs={{0,1},{1,0},{2,3},{3,2},{4,5},{5,4},{6,7},{7,6},{8,9},{9,8},{10,11... | collective-permute-start | bytes 442376 | tf_op jit(solution)/shard_map/ppermute | solution.py:384
  351.3 42.2 %collective-permute-start.78 = (bf16[4,16,384]{2,1,0:T(8,128)(2,1)S(1)}, bf16[4,16,384]{2,1,0:T(8,128)(2,1)S(1)}, u32[]{:S(2)}, u32[]{:S(2)}) collective-permute-start(bf16[4,16,384]{2,1,0:T(8,128)(2,1)S(1)} %get-tuple-element.637), channel_id=1, source_target_pairs={{0,1},{1,0},{2,3},{3,2},{4,5},{5,4},{6,7},{7,6},{8,9},{9,8},{10,11... | collective-permute-start | bytes 147464 | tf_op jit(solution)/shard_map/ppermute | solution.py:384
  352.0 42.4 %collective-permute-start.80 = (bf16[4,16,384]{2,1,0:T(8,128)(2,1)S(1)}, bf16[4,16,384]{2,1,0:T(8,128)(2,1)S(1)}, u32[]{:S(2)}, u32[]{:S(2)}) collective-permute-start(bf16[4,16,384]{2,1,0:T(8,128)(2,1)S(1)} %get-tuple-element.639), channel_id=1, source_target_pairs={{0,2},{1,3},{2,0},{3,1},{4,6},{5,7},{6,4},{7,5},{8,10},{9,11},{10,... | collective-permute-start | bytes 147464 | tf_op jit(solution)/shard_map/ppermute | solution.py:384
  454.3 36.1 %collective-permute-start.72 = (bf16[4,64,384]{2,1,0:T(8,128)(2,1)}, bf16[4,64,384]{2,1,0:T(8,128)(2,1)S(1)}, u32[]{:S(2)}, u32[]{:S(2)}) collective-permute-start(bf16[4,64,384]{2,1,0:T(8,128)(2,1)} %copy-done.2), channel_id=1, source_target_pairs={{0,3},{1,2},{2,1},{3,0},{4,7},{5,6},{6,5},{7,4},{8,11},{9,10},{10,... | collective-permute-start | bytes 589832 | tf_op jit(solution)/shard_map/ppermute | solution.py:384
  454.5 36.0 %collective-permute-start.73 = (bf16[4,64,384]{2,1,0:T(8,128)(2,1)}, bf16[4,64,384]{2,1,0:T(8,128)(2,1)S(1)}, u32[]{:S(2)}, u32[]{:S(2)}) collective-permute-start(bf16[4,64,384]{2,1,0:T(8,128)(2,1)} %copy-done.3), channel_id=1, source_target_pairs={{0,4},{1,5},{2,6},{3,7},{4,0},{5,1},{6,2},{7,3},{8,12},{9,13},{10,... | collective-permute-start | bytes 589832 | tf_op jit(solution)/shard_map/ppermute | solution.py:384
  456.3 37.1 %collective-permute-start.74 = (bf16[4,64,384]{2,1,0:T(8,128)(2,1)}, bf16[4,64,384]{2,1,0:T(8,128)(2,1)S(1)}, u32[]{:S(2)}, u32[]{:S(2)}) collective-permute-start(bf16[4,64,384]{2,1,0:T(8,128)(2,1)} %copy-done.4), channel_id=1, source_target_pairs={{0,5},{1,4},{2,7},{3,6},{4,1},{5,0},{6,3},{7,2},{8,13},{9,12},{10,... | collective-permute-start | bytes 589832 | tf_op jit(solution)/shard_map/ppermute | solution.py:384
  457.2 36.6 %collective-permute-start.75 = (bf16[4,64,384]{2,1,0:T(8,128)(2,1)}, bf16[4,64,384]{2,1,0:T(8,128)(2,1)S(1)}, u32[]{:S(2)}, u32[]{:S(2)}) collective-permute-start(bf16[4,64,384]{2,1,0:T(8,128)(2,1)} %copy-done.5), channel_id=1, source_target_pairs={{0,6},{1,7},{2,4},{3,5},{4,2},{5,3},{6,0},{7,1},{8,14},{9,15},{10,... | collective-permute-start | bytes 589832 | tf_op jit(solution)/shard_map/ppermute | solution.py:384
  493.4 31.0 %collective-permute-start.67 = (bf16[4,64,384]{2,1,0:T(8,128)(2,1)S(1)}, bf16[4,64,384]{2,1,0:T(8,128)(2,1)S(1)}, u32[]{:S(2)}, u32[]{:S(2)}) collective-permute-start(bf16[4,64,384]{2,1,0:T(8,128)(2,1)S(1)} %copy-done.14), channel_id=1, source_target_pairs={{0,5},{1,4},{2,7},{3,6},{4,1},{5,0},{6,3},{7,2},{8,13},{9,12},{10,... | collective-permute-start | bytes 589832 | tf_op jit(solution)/shard_map/ppermute | solution.py:384
  506.2 31.1 %collective-permute-start.58 = (bf16[4,64,384]{2,1,0:T(8,128)(2,1)S(1)}, bf16[4,64,384]{2,1,0:T(8,128)(2,1)S(1)}, u32[]{:S(2)}, u32[]{:S(2)}) collective-permute-start(bf16[4,64,384]{2,1,0:T(8,128)(2,1)S(1)} %copy-done.22), channel_id=1, source_target_pairs={{0,3},{1,2},{2,1},{3,0},{4,7},{5,6},{6,5},{7,4},{8,11},{9,10},{10,... | collective-permute-start | bytes 589832 | tf_op jit(solution)/shard_map/ppermute | solution.py:384
  516.3 40.2 %collective-permute-start.59 = (bf16[4,64,384]{2,1,0:T(8,128)(2,1)S(1)}, bf16[4,64,384]{2,1,0:T(8,128)(2,1)S(1)}, u32[]{:S(2)}, u32[]{:S(2)}) collective-permute-start(bf16[4,64,384]{2,1,0:T(8,128)(2,1)S(1)} %copy-done.24), channel_id=1, source_target_pairs={{0,4},{1,5},{2,6},{3,7},{4,0},{5,1},{6,2},{7,3},{8,12},{9,13},{10,... | collective-permute-start | bytes 589832 | tf_op jit(solution)/shard_map/ppermute | solution.py:384
  524.4 32.6 %collective-permute-start.60 = (bf16[4,64,384]{2,1,0:T(8,128)(2,1)S(1)}, bf16[4,64,384]{2,1,0:T(8,128)(2,1)S(1)}, u32[]{:S(2)}, u32[]{:S(2)}) collective-permute-start(bf16[4,64,384]{2,1,0:T(8,128)(2,1)S(1)} %copy-done.26), channel_id=1, source_target_pairs={{0,5},{1,4},{2,7},{3,6},{4,1},{5,0},{6,3},{7,2},{8,13},{9,12},{10,... | collective-permute-start | bytes 589832 | tf_op jit(solution)/shard_map/ppermute | solution.py:384
  524.4 34.4 %collective-permute-start.61 = (bf16[4,64,384]{2,1,0:T(8,128)(2,1)S(1)}, bf16[4,64,384]{2,1,0:T(8,128)(2,1)S(1)}, u32[]{:S(2)}, u32[]{:S(2)}) collective-permute-start(bf16[4,64,384]{2,1,0:T(8,128)(2,1)S(1)} %copy-done.28), channel_id=1, source_target_pairs={{0,6},{1,7},{2,4},{3,5},{4,2},{5,3},{6,0},{7,1},{8,14},{9,15},{10,... | collective-permute-start | bytes 589832 | tf_op jit(solution)/shard_map/ppermute | solution.py:384
  526.4 34.4 %collective-permute-start.62 = (bf16[4,64,384]{2,1,0:T(8,128)(2,1)S(1)}, bf16[4,64,384]{2,1,0:T(8,128)(2,1)S(1)}, u32[]{:S(2)}, u32[]{:S(2)}) collective-permute-start(bf16[4,64,384]{2,1,0:T(8,128)(2,1)S(1)} %copy-done.30), channel_id=1, source_target_pairs={{0,7},{1,6},{2,5},{3,4},{4,3},{5,2},{6,1},{7,0},{8,15},{9,14},{10,... | collective-permute-start | bytes 589832 | tf_op jit(solution)/shard_map/ppermute | solution.py:384
  537.4 35.2 %collective-permute-start.51 = (bf16[4,64,384]{2,1,0:T(8,128)(2,1)S(1)}, bf16[4,64,384]{2,1,0:T(8,128)(2,1)S(1)}, u32[]{:S(2)}, u32[]{:S(2)}) collective-permute-start(bf16[4,64,384]{2,1,0:T(8,128)(2,1)S(1)} %copy-done.34), channel_id=1, source_target_pairs={{0,3},{1,2},{2,1},{3,0},{4,7},{5,6},{6,5},{7,4},{8,11},{9,10},{10,... | collective-permute-start | bytes 589832 | tf_op jit(solution)/shard_map/ppermute | solution.py:384
  557.0 34.8 %collective-permute-start.53 = (bf16[4,64,384]{2,1,0:T(8,128)(2,1)S(1)}, bf16[4,64,384]{2,1,0:T(8,128)(2,1)S(1)}, u32[]{:S(2)}, u32[]{:S(2)}) collective-permute-start(bf16[4,64,384]{2,1,0:T(8,128)(2,1)S(1)} %copy-done.38), channel_id=1, source_target_pairs={{0,5},{1,4},{2,7},{3,6},{4,1},{5,0},{6,3},{7,2},{8,13},{9,12},{10,... | collective-permute-start | bytes 589832 | tf_op jit(solution)/shard_map/ppermute | solution.py:384
  558.8 33.0 %collective-permute-start.54 = (bf16[4,64,384]{2,1,0:T(8,128)(2,1)S(1)}, bf16[4,64,384]{2,1,0:T(8,128)(2,1)S(1)}, u32[]{:S(2)}, u32[]{:S(2)}) collective-permute-start(bf16[4,64,384]{2,1,0:T(8,128)(2,1)S(1)} %copy-done.40), channel_id=1, source_target_pairs={{0,6},{1,7},{2,4},{3,5},{4,2},{5,3},{6,0},{7,1},{8,14},{9,15},{10,... | collective-permute-start | bytes 589832 | tf_op jit(solution)/shard_map/ppermute | solution.py:384
  560.8 33.1 %collective-permute-start.55 = (bf16[4,64,384]{2,1,0:T(8,128)(2,1)S(1)}, bf16[4,64,384]{2,1,0:T(8,128)(2,1)S(1)}, u32[]{:S(2)}, u32[]{:S(2)}) collective-permute-start(bf16[4,64,384]{2,1,0:T(8,128)(2,1)S(1)} %copy-done.42), channel_id=1, source_target_pairs={{0,7},{1,6},{2,5},{3,4},{4,3},{5,2},{6,1},{7,0},{8,15},{9,14},{10,... | collective-permute-start | bytes 589832 | tf_op jit(solution)/shard_map/ppermute | solution.py:384
  572.6 32.6 %collective-permute-start.44 = (bf16[4,64,384]{2,1,0:T(8,128)(2,1)S(1)}, bf16[4,64,384]{2,1,0:T(8,128)(2,1)S(1)}, u32[]{:S(2)}, u32[]{:S(2)}) collective-permute-start(bf16[4,64,384]{2,1,0:T(8,128)(2,1)S(1)} %copy-done.46), channel_id=1, source_target_pairs={{0,3},{1,2},{2,1},{3,0},{4,7},{5,6},{6,5},{7,4},{8,11},{9,10},{10,... | collective-permute-start | bytes 589832 | tf_op jit(solution)/shard_map/ppermute | solution.py:384
  583.7 40.5 %collective-permute-start.45 = (bf16[4,64,384]{2,1,0:T(8,128)(2,1)S(1)}, bf16[4,64,384]{2,1,0:T(8,128)(2,1)S(1)}, u32[]{:S(2)}, u32[]{:S(2)}) collective-permute-start(bf16[4,64,384]{2,1,0:T(8,128)(2,1)S(1)} %copy-done.48), channel_id=1, source_target_pairs={{0,4},{1,5},{2,6},{3,7},{4,0},{5,1},{6,2},{7,3},{8,12},{9,13},{10,... | collective-permute-start | bytes 589832 | tf_op jit(solution)/shard_map/ppermute | solution.py:384
  591.9 32.9 %collective-permute-start.46 = (bf16[4,64,384]{2,1,0:T(8,128)(2,1)S(1)}, bf16[4,64,384]{2,1,0:T(8,128)(2,1)S(1)}, u32[]{:S(2)}, u32[]{:S(2)}) collective-permute-start(bf16[4,64,384]{2,1,0:T(8,128)(2,1)S(1)} %copy-done.50), channel_id=1, source_target_pairs={{0,5},{1,4},{2,7},{3,6},{4,1},{5,0},{6,3},{7,2},{8,13},{9,12},{10,... | collective-permute-start | bytes 589832 | tf_op jit(solution)/shard_map/ppermute | solution.py:384
  591.9 34.7 %collective-permute-start.47 = (bf16[4,64,384]{2,1,0:T(8,128)(2,1)S(1)}, bf16[4,64,384]{2,1,0:T(8,128)(2,1)S(1)}, u32[]{:S(2)}, u32[]{:S(2)}) collective-permute-start(bf16[4,64,384]{2,1,0:T(8,128)(2,1)S(1)} %copy-done.52), channel_id=1, source_target_pairs={{0,6},{1,7},{2,4},{3,5},{4,2},{5,3},{6,0},{7,1},{8,14},{9,15},{10,... | collective-permute-start | bytes 589832 | tf_op jit(solution)/shard_map/ppermute | solution.py:384
  593.9 34.7 %collective-permute-start.48 = (bf16[4,64,384]{2,1,0:T(8,128)(2,1)S(1)}, bf16[4,64,384]{2,1,0:T(8,128)(2,1)S(1)}, u32[]{:S(2)}, u32[]{:S(2)}) collective-permute-start(bf16[4,64,384]{2,1,0:T(8,128)(2,1)S(1)} %copy-done.54), channel_id=1, source_target_pairs={{0,7},{1,6},{2,5},{3,4},{4,3},{5,2},{6,1},{7,0},{8,15},{9,14},{10,... | collective-permute-start | bytes 589832 | tf_op jit(solution)/shard_map/ppermute | solution.py:384
  605.2 35.2 %collective-permute-start.37 = (bf16[4,64,384]{2,1,0:T(8,128)(2,1)S(1)}, bf16[4,64,384]{2,1,0:T(8,128)(2,1)S(1)}, u32[]{:S(2)}, u32[]{:S(2)}) collective-permute-start(bf16[4,64,384]{2,1,0:T(8,128)(2,1)S(1)} %copy-done.56), channel_id=1, source_target_pairs={{0,3},{1,2},{2,1},{3,0},{4,7},{5,6},{6,5},{7,4},{8,11},{9,10},{10,... | collective-permute-start | bytes 589832 | tf_op jit(solution)/shard_map/ppermute | solution.py:384
  624.8 34.5 %collective-permute-start.39 = (bf16[4,64,384]{2,1,0:T(8,128)(2,1)S(1)}, bf16[4,64,384]{2,1,0:T(8,128)(2,1)S(1)}, u32[]{:S(2)}, u32[]{:S(2)}) collective-permute-start(bf16[4,64,384]{2,1,0:T(8,128)(2,1)S(1)} %copy-done.60), channel_id=1, source_target_pairs={{0,5},{1,4},{2,7},{3,6},{4,1},{5,0},{6,3},{7,2},{8,13},{9,12},{10,... | collective-permute-start | bytes 589832 | tf_op jit(solution)/shard_map/ppermute | solution.py:384
  626.6 32.7 %collective-permute-start.40 = (bf16[4,64,384]{2,1,0:T(8,128)(2,1)S(1)}, bf16[4,64,384]{2,1,0:T(8,128)(2,1)S(1)}, u32[]{:S(2)}, u32[]{:S(2)}) collective-permute-start(bf16[4,64,384]{2,1,0:T(8,128)(2,1)S(1)} %copy-done.62), channel_id=1, source_target_pairs={{0,6},{1,7},{2,4},{3,5},{4,2},{5,3},{6,0},{7,1},{8,14},{9,15},{10,... | collective-permute-start | bytes 589832 | tf_op jit(solution)/shard_map/ppermute | solution.py:384
  628.6 32.7 %collective-permute-start.41 = (bf16[4,64,384]{2,1,0:T(8,128)(2,1)S(1)}, bf16[4,64,384]{2,1,0:T(8,128)(2,1)S(1)}, u32[]{:S(2)}, u32[]{:S(2)}) collective-permute-start(bf16[4,64,384]{2,1,0:T(8,128)(2,1)S(1)} %copy-done.64), channel_id=1, source_target_pairs={{0,7},{1,6},{2,5},{3,4},{4,3},{5,2},{6,1},{7,0},{8,15},{9,14},{10,... | collective-permute-start | bytes 589832 | tf_op jit(solution)/shard_map/ppermute | solution.py:384
  640.5 32.3 %collective-permute-start.30 = (bf16[4,64,384]{2,1,0:T(8,128)(2,1)S(1)}, bf16[4,64,384]{2,1,0:T(8,128)(2,1)S(1)}, u32[]{:S(2)}, u32[]{:S(2)}) collective-permute-start(bf16[4,64,384]{2,1,0:T(8,128)(2,1)S(1)} %copy-done.66), channel_id=1, source_target_pairs={{0,3},{1,2},{2,1},{3,0},{4,7},{5,6},{6,5},{7,4},{8,11},{9,10},{10,... | collective-permute-start | bytes 589832 | tf_op jit(solution)/shard_map/ppermute | solution.py:384
  651.2 33.6 %collective-permute-start.31 = (bf16[4,64,384]{2,1,0:T(8,128)(2,1)S(1)}, bf16[4,64,384]{2,1,0:T(8,128)(2,1)S(1)}, u32[]{:S(2)}, u32[]{:S(2)}) collective-permute-start(bf16[4,64,384]{2,1,0:T(8,128)(2,1)S(1)} %copy-done.68), channel_id=1, source_target_pairs={{0,4},{1,5},{2,6},{3,7},{4,0},{5,1},{6,2},{7,3},{8,12},{9,13},{10,... | collective-permute-start | bytes 589832 | tf_op jit(solution)/shard_map/ppermute | solution.py:384
  659.4 32.6 %collective-permute-start.33 = (bf16[4,64,384]{2,1,0:T(8,128)(2,1)S(1)}, bf16[4,64,384]{2,1,0:T(8,128)(2,1)S(1)}, u32[]{:S(2)}, u32[]{:S(2)}) collective-permute-start(bf16[4,64,384]{2,1,0:T(8,128)(2,1)S(1)} %copy-done.72), channel_id=1, source_target_pairs={{0,6},{1,7},{2,4},{3,5},{4,2},{5,3},{6,0},{7,1},{8,14},{9,15},{10,... | collective-permute-start | bytes 589832 | tf_op jit(solution)/shard_map/ppermute | solution.py:384
  661.3 31.9 %collective-permute-start.34 = (bf16[4,64,384]{2,1,0:T(8,128)(2,1)S(1)}, bf16[4,64,384]{2,1,0:T(8,128)(2,1)S(1)}, u32[]{:S(2)}, u32[]{:S(2)}) collective-permute-start(bf16[4,64,384]{2,1,0:T(8,128)(2,1)S(1)} %copy-done.74), channel_id=1, source_target_pairs={{0,7},{1,6},{2,5},{3,4},{4,3},{5,2},{6,1},{7,0},{8,15},{9,14},{10,... | collective-permute-start | bytes 589832 | tf_op jit(solution)/shard_map/ppermute | solution.py:384
  732.0 33.0 %collective-permute-start.110 = (bf16[1,512,384]{2,1,0:T(8,128)(2,1)S(1)}, bf16[1,512,384]{2,1,0:T(8,128)(2,1)S(1)}, u32[]{:S(2)}, u32[]{:S(2)}) collective-permute-start(bf16[1,512,384]{2,1,0:T(8,128)(2,1)S(1)} %get-tuple-element.684), channel_id=1, source_target_pairs={{0,16},{8,24},{16,0},{24,8},{1,17},{9,25},{17,1},{25,9},{2,18},{10... | collective-permute-start | bytes 1179656 | tf_op jit(solution)/shard_map/ppermute | solution.py:384
  767.9 39.2 %collective-permute-start.116 = (bf16[1,512,384]{2,1,0:T(8,128)(2,1)}, bf16[1,512,384]{2,1,0:T(8,128)(2,1)}, u32[]{:S(2)}, u32[]{:S(2)}) collective-permute-start(bf16[1,512,384]{2,1,0:T(8,128)(2,1)} %get-tuple-element.694), channel_id=1, source_target_pairs={{0,16},{8,24},{16,0},{24,8},{1,17},{9,25},{17,1},{25,9},{2,18},{10... | collective-permute-start | bytes 1179656 | tf_op jit(solution)/shard_map/ppermute | solution.py:384
  777.2 56.3 %collective-permute-start.102 = (bf16[1,512,384]{2,1,0:T(8,128)(2,1)S(1)}, bf16[1,512,384]{2,1,0:T(8,128)(2,1)S(1)}, u32[]{:S(2)}, u32[]{:S(2)}) collective-permute-start(bf16[1,512,384]{2,1,0:T(8,128)(2,1)S(1)} %copy-done.196), channel_id=1, source_target_pairs={{0,24},{8,16},{16,8},{24,0},{1,25},{9,17},{17,9},{25,1},{2,26},{10... | collective-permute-start | bytes 1179656 | tf_op jit(solution)/shard_map/ppermute | solution.py:384
  781.9 43.8 %collective-permute-start.117 = (bf16[1,512,384]{2,1,0:T(8,128)(2,1)S(1)}, bf16[1,512,384]{2,1,0:T(8,128)(2,1)S(1)}, u32[]{:S(2)}, u32[]{:S(2)}) collective-permute-start(bf16[1,512,384]{2,1,0:T(8,128)(2,1)S(1)} %copy-done.198), channel_id=1, source_target_pairs={{0,24},{8,16},{16,8},{24,0},{1,25},{9,17},{17,9},{25,1},{2,26},{10... | collective-permute-start | bytes 1179656 | tf_op jit(solution)/shard_map/ppermute | solution.py:384
  784.3 50.7 %collective-permute-start.118 = (bf16[1,512,384]{2,1,0:T(8,128)(2,1)S(1)}, bf16[1,512,384]{2,1,0:T(8,128)(2,1)S(1)}, u32[]{:S(2)}, u32[]{:S(2)}) collective-permute-start(bf16[1,512,384]{2,1,0:T(8,128)(2,1)S(1)} %get-tuple-element.697), channel_id=1, source_target_pairs={{0,8},{8,0},{16,24},{24,16},{1,9},{9,1},{17,25},{25,17},{2,10},{10... | collective-permute-start | bytes 1179656 | tf_op jit(solution)/shard_map/ppermute | solution.py:384
  787.0 49.5 %collective-permute-start.119 = (bf16[1,512,384]{2,1,0:T(8,128)(2,1)S(1)}, bf16[1,512,384]{2,1,0:T(8,128)(2,1)S(1)}, u32[]{:S(2)}, u32[]{:S(2)}) collective-permute-start(bf16[1,512,384]{2,1,0:T(8,128)(2,1)S(1)} %get-tuple-element.698), channel_id=1, source_target_pairs={{0,16},{8,24},{16,0},{24,8},{1,17},{9,25},{17,1},{25,9},{2,18},{10... | collective-permute-start | bytes 1179656 | tf_op jit(solution)/shard_map/ppermute | solution.py:384
  840.1 45.0 %collective-permute-start.125 = (bf16[1,512,384]{2,1,0:T(8,128)(2,1)S(1)}, bf16[1,512,384]{2,1,0:T(8,128)(2,1)S(1)}, u32[]{:S(2)}, u32[]{:S(2)}) collective-permute-start(bf16[1,512,384]{2,1,0:T(8,128)(2,1)S(1)} %get-tuple-element.706), channel_id=1, source_target_pairs={{0,16},{8,24},{16,0},{24,8},{1,17},{9,25},{17,1},{25,9},{2,18},{10... | collective-permute-start | bytes 1179656 | tf_op jit(solution)/shard_map/ppermute | solution.py:384
  847.9 40.2 %collective-permute-start.96 = (bf16[1,512,384]{2,1,0:T(8,128)(2,1)S(1)}, bf16[1,512,384]{2,1,0:T(8,128)(2,1)S(1)}, u32[]{:S(2)}, u32[]{:S(2)}) collective-permute-start(bf16[1,512,384]{2,1,0:T(8,128)(2,1)S(1)} %copy-done.192), channel_id=1, source_target_pairs={{0,24},{8,16},{16,8},{24,0},{1,25},{9,17},{17,9},{25,1},{2,26},{10... | collective-permute-start | bytes 1179656 | tf_op jit(solution)/shard_map/ppermute | solution.py:384
  865.3 36.6 %collective-permute-start.128 = (bf16[1,512,384]{2,1,0:T(8,128)(2,1)S(1)}, bf16[1,512,384]{2,1,0:T(8,128)(2,1)S(1)}, u32[]{:S(2)}, u32[]{:S(2)}) collective-permute-start(bf16[1,512,384]{2,1,0:T(8,128)(2,1)S(1)} %get-tuple-element.710), channel_id=1, source_target_pairs={{0,16},{8,24},{16,0},{24,8},{1,17},{9,25},{17,1},{25,9},{2,18},{10... | collective-permute-start | bytes 1179656 | tf_op jit(solution)/shard_map/ppermute | solution.py:384
  920.7 31.8 %collective-permute-start.134 = (bf16[1,512,384]{2,1,0:T(8,128)(2,1)S(1)}, bf16[1,512,384]{2,1,0:T(8,128)(2,1)S(1)}, u32[]{:S(2)}, u32[]{:S(2)}) collective-permute-start(bf16[1,512,384]{2,1,0:T(8,128)(2,1)S(1)} %get-tuple-element.717), channel_id=1, source_target_pairs={{0,16},{8,24},{16,0},{24,8},{1,17},{9,25},{17,1},{25,9},{2,18},{10... | collective-permute-start | bytes 1179656 | tf_op jit(solution)/shard_map/ppermute | solution.py:384
  (280 other events, 4678.3 us)
